TPU v7x, 256 devices: a whole 4x4x8 slice. The times are simulated.
256 devices in a mesh: lat: 4 (over x_lo, core), wide: 64 (over x_hi, z, y).
Axes of the slice: x: 4 (x_hi: 2, x_lo: 2; x = x_hi * 2 + x_lo), y: 4, z: 8, core: 2. Of those that a mesh axis runs over, the one named last changes fastest.
Arguments:
- fields: float32 [4, 128, 128, 256], P(None, 'wide', 'lat'), may hold values from -4 to 4
- w_first: bfloat16 [3, 4, 64], replicated, may hold values from -1.75 to 1.75
- w_second: bfloat16 [3, 64, 64], replicated, may hold values from -0.4375 to 0.4375
- w_third: bfloat16 [3, 64, 64], replicated, may hold values from -0.4375 to 0.4375
- w_last: bfloat16 [3, 64, 4], replicated, may hold values from -0.4375 to 0.4375
Outputs:
- stepped: float32 [4, 128, 128, 256], P(None, 'wide', 'lat')
All inputs are finite; a program needn't handle non-finite values.
Results may differ from a plain program's by a relative error of at most 0.0056.
Values may be sent and summed in bfloat16 or wider, within the bound.
A program may use at most 64 MiB of HBM per device.

v0:
```python
import jax
import jax.numpy as jnp
from jax import lax
from jax.sharding import PartitionSpec as P

courant = 0.3
smooth_eps = 0.01


def padded_2(block, sides, width):
    for axis, dim in sides:
        count = lax.axis_size(axis)
        forward = [(i, i + 1) for i in range(count - 1)]
        backward = [(target, source) for source, target in forward]
        low = lax.ppermute(
            lax.slice_in_dim(block, block.shape[dim] - width, None, axis=dim), axis, forward
        )
        high = lax.ppermute(lax.slice_in_dim(block, 0, width, axis=dim), axis, backward)
        block = jnp.concatenate([low, block, high], axis=dim)
    return block


def smooth_abs(values):
    return jnp.sqrt(values * values + smooth_eps)


def advect(extended, at_south, at_north):
    cells = extended[:, :, 1:-1, :]
    east_wind = cells[0]
    east_face = 0.5 * (east_wind + jnp.roll(east_wind, -1, axis=2))
    neighbour = jnp.roll(cells, -1, axis=3)
    east_flux = 0.5 * east_face * (cells + neighbour) - 0.5 * smooth_abs(east_face) * (
        neighbour - cells
    )
    east_div = east_flux - jnp.roll(east_flux, 1, axis=3)
    north_wind = extended[1]
    north_face = 0.5 * (north_wind[:, :-1] + north_wind[:, 1:])
    below_rows = extended[:, :, :-1]
    above_rows = extended[:, :, 1:]
    north_flux = 0.5 * north_face * (below_rows + above_rows) - 0.5 * smooth_abs(north_face) * (
        above_rows - below_rows
    )
    n_faces = north_flux.shape[2]
    row_index = lax.broadcasted_iota(jnp.int32, (1, 1, n_faces, 1), 2)
    closed = jnp.logical_or(
        jnp.logical_and(row_index == 0, at_south),
        jnp.logical_and(row_index == n_faces - 1, at_north),
    )
    north_flux = jnp.where(closed, jnp.float32(0.0), north_flux)
    north_div = north_flux[:, :, 1:] - north_flux[:, :, :-1]
    return cells - courant * (east_div + north_div)


def conv_levels(inputs, kernel):
    padded = jnp.pad(inputs, ((0, 0), (0, 0), (1, 1)))
    n_lev = inputs.shape[2]
    result = jnp.einsum(
        "cbl,co->obl", padded[:, :, 0:n_lev], kernel[0], preferred_element_type=jnp.float32
    )
    result = result + jnp.einsum(
        "cbl,co->obl", padded[:, :, 1 : 1 + n_lev], kernel[1], preferred_element_type=jnp.float32
    )
    result = result + jnp.einsum(
        "cbl,co->obl", padded[:, :, 2 : 2 + n_lev], kernel[2], preferred_element_type=jnp.float32
    )
    return result


def column_net(columns, weights):
    n_fields, n_lev, n_rows, n_lon = columns.shape
    inputs = jnp.transpose(columns, (0, 3, 2, 1)).reshape(n_fields, n_lon * n_rows, n_lev)
    hidden = jax.nn.silu(conv_levels(inputs, weights[0])).astype(jnp.bfloat16)
    hidden = (hidden.astype(jnp.float32) + jax.nn.silu(conv_levels(hidden, weights[1]))).astype(
        jnp.bfloat16
    )
    hidden = (hidden.astype(jnp.float32) + jax.nn.silu(conv_levels(hidden, weights[2]))).astype(
        jnp.bfloat16
    )
    result = conv_levels(hidden, weights[3])
    result = result.reshape(n_fields, n_lon, n_rows, n_lev)
    return jnp.transpose(result, (0, 3, 2, 1))


def on_device(fields, w_first, w_second, w_third, w_last):
    band_count = lax.axis_size("lat")
    band_index = lax.axis_index("lat")
    at_south = band_index == 0
    at_north = band_index == band_count - 1
    weights = (w_first, w_second, w_third, w_last)
    extended = padded_2(fields, (("lat", 2),), 1)
    advected = advect(extended, at_south, at_north)
    packed = advected.astype(jnp.bfloat16)
    columns = lax.all_to_all(packed, "wide", split_axis=3, concat_axis=1, tiled=True)
    column_tend = column_net(columns, weights)
    tendency = lax.all_to_all(column_tend, "wide", split_axis=1, concat_axis=3, tiled=True)
    updated = advected + tendency
    extended_two = padded_2(updated, (("lat", 2),), 1)
    return advect(extended_two, at_south, at_north)


def solution(mesh):
    return jax.shard_map(
        on_device,
        mesh=mesh,
        in_specs=(P(None, "wide", "lat", None), P(), P(), P(), P()),
        out_specs=P(None, "wide", "lat", None),
        check_vma=False,
    )
```

profile of v0, /device:TPU:1, one launch (start us, length us, event | category | flops | bytes accessed | tf_op | source)
XLA Modules:
  0.0 85.7 jit_solution(14320944566279273832)
XLA Ops:
  0.0 1.2 %copy.166 = f32[4,2,32,256]{3,0,2,1:T(4,128)S(1)} copy(f32[4,2,32,256]{3,2,1,0:T(8,128)} %param.5) | data formatting | bytes 524288 | tf_op args[0]
  1.2 4.5 %collective-permute-start = (f32[4,2,1,256]{3,0,2,1:T(4,128)S(1)}, f32[4,2,1,256]{3,0,2,1:T(4,128)S(1)}, u32[]{:S(2)}, u32[]{:S(2)}) collective-permute-start(f32[4,2,1,256]{3,0,2,1:T(4,128)S(1)} %get-tuple-element.16), channel_id=1, source_target_pairs={{0,64},{64,128},{128,192},{1,65},{65,129},{129,193},{2,66},{66,130... | collective-permute-start | bytes 24584 | tf_op jit(solution)/shard_map/ppermute | solution.py:15
  5.7 1.9 %collective-permute-start.1 = (f32[4,2,1,256]{3,0,2,1:T(4,128)S(1)}, f32[4,2,1,256]{3,0,2,1:T(4,128)S(1)}, u32[]{:S(2)}, u32[]{:S(2)}) collective-permute-start(f32[4,2,1,256]{3,0,2,1:T(4,128)S(1)} %get-tuple-element.17), channel_id=1, source_target_pairs={{64,0},{128,64},{192,128},{65,1},{129,65},{193,129},{66,2},{130,66... | collective-permute-start | bytes 24584 | tf_op jit(solution)/shard_map/ppermute | solution.py:18
  7.6 0.9 %slice.166 = f32[4,2,32,1]{3,2,1,0:T(8,128)S(1)} slice(f32[4,2,32,256]{3,2,1,0:T(8,128)} %param.5), slice={[0:4], [0:2], [0:32], [0:1]} | slice | bytes 2048 | tf_op jit(solution)/shard_map/jit(_roll_static)/slice | solution.py:31
  8.6 1.1 %slice.165 = f32[4,2,32,255]{3,2,1,0:T(8,128)S(1)} slice(f32[4,2,32,256]{3,2,1,0:T(8,128)} %param.5), slice={[0:4], [0:2], [0:32], [1:256]} | slice | bytes 522240 | tf_op jit(solution)/shard_map/jit(_roll_static)/slice | solution.py:31
  9.6 1.2 %copy.174 = f32[4,2,32,256]{3,1,2,0:T(2,128)S(1)} copy(f32[4,2,32,256]{3,2,1,0:T(8,128)} %param.5) | data formatting | bytes 524288 | tf_op args[0]
  14.4 25.7 %all_to_all.36 = bf16[64,2,512]{2,1,0:T(2,128)(2,1)S(1)} all-to-all(bf16[64,2,512]{2,1,0:T(2,128)(2,1)S(1)} %reshape.47), channel_id=1, replica_groups=mesh['lat'=4,'wide'=64] {'wide'}, dimensions={0} | all-to-all | bytes 262144 | tf_op jit(solution)/shard_map/all_to_all | solution.py:93
  41.2 0.8 fusion.26
  41.9 0.7 fusion.47
  42.7 1.7 %fusion.11 = bf16[64,128,128]{2,0,1:T(8,128)(2,1)S(1)} fusion(f32[128,128,64]{1,2,0:T(8,128)S(1)} %fusion.26, f32[128,128,64]{1,2,0:T(8,128)S(1)} %fusion.47, bf16[4,128,128]{2,0,1:T(4,128)(2,1)S(1)} %bitcast.158, bf16[3,4,64]{2,1,0:T(4,128)(2,1)S(1)} %copy-done.4), kind=kOutput, calls=%fused_computation.23 | convolution fusion | flops 15728640 | bytes 10617856 | tf_op jit(solution)/shard_map/cbl,co->obl/dot_general | solution.py:63
  44.4 0.8 fusion.14
  45.2 0.7 fusion.33
  46.0 2.1 %fusion.12 = bf16[64,128,128]{2,0,1:T(8,128)(2,1)S(1)} fusion(f32[128,128,64]{1,2,0:T(8,128)S(1)} %fusion.14, f32[128,128,64]{1,2,0:T(8,128)S(1)} %fusion.33, bf16[64,128,128]{2,0,1:T(8,128)(2,1)S(1)} %fusion.11, bf16[3,64,64]{2,1,0:T(8,128)(2,1)S(1)} %copy-done.1), kind=kOutput, calls=%fused_computation.24 | convolution fusion | flops 143654912 | bytes 14696448 | tf_op jit(solution)/shard_map/cbl,co->obl/dot_general | solution.py:63
  48.1 0.8 fusion.15
  48.9 0.7 fusion.29
  49.7 2.1 %fusion.13 = bf16[64,128,128]{2,0,1:T(8,128)(2,1)S(1)} fusion(f32[128,128,64]{1,2,0:T(8,128)S(1)} %fusion.15, f32[128,128,64]{1,2,0:T(8,128)S(1)} %fusion.29, bf16[64,128,128]{2,0,1:T(8,128)(2,1)S(1)} %fusion.12, bf16[3,64,64]{2,1,0:T(8,128)(2,1)S(1)} %copy-done.2), kind=kOutput, calls=%fused_computation.25 | convolution fusion | flops 143654912 | bytes 14696448 | tf_op jit(solution)/shard_map/cbl,co->obl/dot_general | solution.py:63
  52.2 0.7 fusion.19
  52.9 0.7 fusion.18
  55.1 16.9 %all_to_all.37 = f32[64,1,1024]{2,1,0:T(1,128)S(1)} all-to-all(f32[64,1,1024]{2,1,0:T(1,128)S(1)} %reshape.49), channel_id=1, replica_groups=mesh['lat'=4,'wide'=64] {'wide'}, dimensions={0} | all-to-all | bytes 524288 | tf_op jit(solution)/shard_map/all_to_all | solution.py:95
  72.5 1.3 %reduce = f32[64,1024]{1,0:T(8,128)S(1)} reduce(f32[64,1,1024]{2,1,0:T(1,128)S(1)} %all_to_all.37, f32[]{:T(128)} %broadcast.89), dimensions={1}, to_apply=%all_to_all.30.reduce_sub_computation | reduce | bytes 524292 | tf_op jit(solution)/shard_map/all_to_all | solution.py:95
  74.7 0.7 copy.187
  76.4 4.4 %collective-permute-start.3 = (f32[4,2,1,256]{3,0,2,1:T(4,128)S(1)}, f32[4,2,1,256]{3,0,2,1:T(4,128)S(1)}, u32[]{:S(2)}, u32[]{:S(2)}) collective-permute-start(f32[4,2,1,256]{3,0,2,1:T(4,128)S(1)} %copy.192), channel_id=1, source_target_pairs={{64,0},{128,64},{192,128},{65,1},{129,65},{193,129},{66,2},{130,66... | collective-permute-start | bytes 24584 | tf_op jit(solution)/shard_map/ppermute | solution.py:18
  80.8 2.2 %collective-permute-start.2 = (f32[4,2,1,256]{3,0,2,1:T(4,128)S(1)}, f32[4,2,1,256]{3,0,2,1:T(4,128)S(1)}, u32[]{:S(2)}, u32[]{:S(2)}) collective-permute-start(f32[4,2,1,256]{3,0,2,1:T(4,128)S(1)} %copy.191), channel_id=1, source_target_pairs={{0,64},{64,128},{128,192},{1,65},{65,129},{129,193},{2,66},{66,130... | collective-permute-start | bytes 24584 | tf_op jit(solution)/shard_map/ppermute | solution.py:15
  84.9 0.7 copy.197
  (68 shorter events, 10.5 us)
Async XLA Ops:
  0.0 11.8 %copy-start = (f32[4,2,32,256]{3,2,1,0:T(8,128)S(1)}, f32[4,2,32,256]{3,2,1,0:T(8,128)}, u32[]{:S(2)}) copy-start(f32[4,2,32,256]{3,2,1,0:T(8,128)} %param.5) | copy-start | bytes 786436
  1.2 10.3 %collective-permute-start = (f32[4,2,1,256]{3,0,2,1:T(4,128)S(1)}, f32[4,2,1,256]{3,0,2,1:T(4,128)S(1)}, u32[]{:S(2)}, u32[]{:S(2)}) collective-permute-start(f32[4,2,1,256]{3,0,2,1:T(4,128)S(1)} %get-tuple-element.16), channel_id=1, source_target_pairs={{0,64},{64,128},{128,192},{1,65},{65,129},{129,193},{2,66},{66,130... | collective-permute-start | bytes 24584 | tf_op jit(solution)/shard_map/ppermute | solution.py:15
  5.7 5.8 %collective-permute-start.1 = (f32[4,2,1,256]{3,0,2,1:T(4,128)S(1)}, f32[4,2,1,256]{3,0,2,1:T(4,128)S(1)}, u32[]{:S(2)}, u32[]{:S(2)}) collective-permute-start(f32[4,2,1,256]{3,0,2,1:T(4,128)S(1)} %get-tuple-element.17), channel_id=1, source_target_pairs={{64,0},{128,64},{192,128},{65,1},{129,65},{193,129},{66,2},{130,66... | collective-permute-start | bytes 24584 | tf_op jit(solution)/shard_map/ppermute | solution.py:18
  12.4 28.8 %copy-start.4 = (bf16[3,4,64]{2,1,0:T(4,128)(2,1)S(1)}, bf16[3,4,64]{2,1,0:T(4,128)(2,1)}, u32[]{:S(2)}) copy-start(bf16[3,4,64]{2,1,0:T(4,128)(2,1)} %param.6) | copy-start | bytes 4612
  42.7 1.7 %copy-start.1 = (bf16[3,64,64]{2,1,0:T(8,128)(2,1)S(1)}, bf16[3,64,64]{2,1,0:T(8,128)(2,1)}, u32[]{:S(2)}) copy-start(bf16[3,64,64]{2,1,0:T(8,128)(2,1)} %param.7) | copy-start | bytes 73732
  45.9 2.2 %copy-start.2 = (bf16[3,64,64]{2,1,0:T(8,128)(2,1)S(1)}, bf16[3,64,64]{2,1,0:T(8,128)(2,1)}, u32[]{:S(2)}) copy-start(bf16[3,64,64]{2,1,0:T(8,128)(2,1)} %param.8) | copy-start | bytes 73732
  49.6 2.2 %copy-start.3 = (bf16[3,64,4]{1,2,0:T(4,128)(2,1)S(1)}, bf16[3,64,4]{1,2,0:T(4,128)(2,1)}, u32[]{:S(2)}) copy-start(bf16[3,64,4]{1,2,0:T(4,128)(2,1)} %param.9) | copy-start | bytes 4612
  76.4 7.6 %collective-permute-start.3 = (f32[4,2,1,256]{3,0,2,1:T(4,128)S(1)}, f32[4,2,1,256]{3,0,2,1:T(4,128)S(1)}, u32[]{:S(2)}, u32[]{:S(2)}) collective-permute-start(f32[4,2,1,256]{3,0,2,1:T(4,128)S(1)} %copy.192), channel_id=1, source_target_pairs={{64,0},{128,64},{192,128},{65,1},{129,65},{193,129},{66,2},{130,66... | collective-permute-start | bytes 24584 | tf_op jit(solution)/shard_map/ppermute | solution.py:18
  80.8 3.2 %collective-permute-start.2 = (f32[4,2,1,256]{3,0,2,1:T(4,128)S(1)}, f32[4,2,1,256]{3,0,2,1:T(4,128)S(1)}, u32[]{:S(2)}, u32[]{:S(2)}) collective-permute-start(f32[4,2,1,256]{3,0,2,1:T(4,128)S(1)} %copy.191), channel_id=1, source_target_pairs={{0,64},{64,128},{128,192},{1,65},{65,129},{129,193},{2,66},{66,130... | collective-permute-start | bytes 24584 | tf_op jit(solution)/shard_map/ppermute | solution.py:15
where the time goes:
time: 86 us; the launch traced here: 85.7 us
  blocking collectives  42.6 us (50%)
  starting transfers between devices  13 us (15%)
  local copies, waits for them, and re-layouts  12.4 us (14%)
  matrix products  12.4 us (14%)
  other arithmetic  4.67 us (5%)
    all_to_all x1, blocking collectives, on_device(): lax.all_to_all(packed, 'wide', split_axis=3, concat_axis=1, tiled=True)  25.7 us
    all_to_all x1, blocking collectives, on_device(): lax.all_to_all(column_tend, 'wide', split_axis=1, concat_axis=3, tiled=True)  16.9 us
    dot_general x4, matrix products, conv_levels(): jnp.einsum('cbl,co->obl', padded[:, :, 2:2 + n_lev], kernel[2], preferred...  6.73 us
    ppermute x2, starting transfers between devices, padded_2(): lax.ppermute(lax.slice_in_dim(block, block.shape[dim] - width, None, axis...  6.72 us
    ppermute x2, starting transfers between devices, padded_2(): lax.ppermute(lax.slice_in_dim(block, 0, width, axis=dim), axis, backward)  6.32 us
    unnamed x18, local copies, waits for them, and re-layouts  4.34 us
    dot_general x4, matrix products, conv_levels(): jnp.einsum('cbl,co->obl', padded[:, :, 0:n_lev], kernel[0], preferred_ele...  3.07 us
    dot_general x4, matrix products, conv_levels(): jnp.einsum('cbl,co->obl', padded[:, :, 1:1 + n_lev], kernel[1], preferred...  2.59 us
  transfers between devices with their start and end apart: 4, of which 0 were waited for; matrix products, arithmetic and copies ran while one was open for 6% of the time, Pallas kernels for 0%

commit v1 on v0

v1 whole, which is shorter than its diff:
```python
import jax
import jax.numpy as jnp
from jax import lax
from jax.experimental import pallas as pl
from jax.experimental.pallas import tpu as pltpu
from jax.sharding import PartitionSpec as P

MESH = pl.DeviceIdType.MESH
F32 = jnp.float32
BF16 = jnp.bfloat16

G = 4
R = 9
STARTS = (0, 8, 17, 25)
CH = 3
NCH = R // CH
SLABS = G + 4


def smooth_abs(v):
    return jnp.sqrt(v * v + 0.01)


def spread(v, first):
    sub = lax.broadcasted_iota(jnp.int32, v.shape, 0)
    if first == 0:
        pair = jnp.where(sub < 2, v, pltpu.roll(v, 2, 0))
    else:
        pair = jnp.where(sub < 2, pltpu.roll(v, 6, 0), v)
    return jnp.where(sub < 4, pair, pltpu.roll(pair, 4, 0))


def transport(rows, masks):
    n = len(rows) - 2
    winds = [spread(v, 2) for v in rows]
    fluxes = []
    for j in range(n + 1):
        low, high = rows[j], rows[j + 1]
        face = 0.5 * (winds[j] + winds[j + 1])
        flux = 0.5 * face * (low + high) - 0.5 * smooth_abs(face) * (high - low)
        if j in masks:
            flux = flux * masks[j]
        fluxes.append(flux)
    outs = []
    for j in range(n):
        cell = rows[j + 1]
        lanes = cell.shape[1]
        wind = spread(cell, 0)
        face = 0.5 * (wind + pltpu.roll(wind, lanes - 1, 1))
        after = pltpu.roll(cell, lanes - 1, 1)
        flux = 0.5 * face * (cell + after) - 0.5 * smooth_abs(face) * (after - cell)
        div = flux - pltpu.roll(flux, 1, 1)
        outs.append(cell - 0.3 * (div + (fluxes[j + 1] - fluxes[j])))
    return outs


def act(t):
    return t + t * jnp.tanh(t)


def dot(a, b):
    return jnp.dot(a, b, preferred_element_type=F32)


def kernel(
    f_hbm, w1_ref, w2_ref, w3_ref, w4_ref, out_ref,
    ext, adv, packed, xbuf, tsend, tin, outv, wa, wb2, wb3, wd, stage, h1, h2, h3,
    in_sem, halo_send, halo_recv, x_send, x_recv, t_send, t_recv,
):
    lat = lax.axis_index("lat")
    wide = lax.axis_index("wide")
    n_lat = lax.axis_size("lat")
    n_groups = lax.axis_size("wide") // G
    grp = wide // G
    m = wide % G
    at_south = lat == 0
    at_north = lat == n_lat - 1
    up = m >= 2
    og = jnp.where(up, grp + 1, grp - 1)
    os = jnp.where(up, m - 2, m + G + 2)
    has_other = jnp.logical_and(og >= 0, og < n_groups)

    barrier = pltpu.get_barrier_semaphore()

    def greet(la, wi):
        pl.semaphore_signal(barrier, inc=1, device_id=(la, wi), device_id_type=MESH)

    @pl.when(grp > 0)
    def _():
        for k in (2, 3):
            greet(lat, (grp - 1) * G + k)

    @pl.when(grp < n_groups - 1)
    def _():
        for k in (0, 1):
            greet(lat, (grp + 1) * G + k)

    for k in range(G):
        @pl.when(m != k)
        def _():
            greet(lat, grp * G + k)

    @pl.when(jnp.logical_not(at_south))
    def _():
        greet(lat - 1, wide)

    @pl.when(jnp.logical_not(at_north))
    def _():
        greet(lat + 1, wide)

    loads = []
    for f in range(4):
        for l in range(2):
            loads.append(
                pltpu.make_async_copy(
                    f_hbm.at[f, l], ext.at[pl.ds(2, 32), 2 * f + l], in_sem.at[2 * f + l]
                )
            )
    for c in loads:
        c.start()

    @pl.when(at_south)
    def _():
        ext[0:2] = jnp.zeros((2, 8, 256), F32)

    @pl.when(at_north)
    def _():
        ext[34:36] = jnp.zeros((2, 8, 256), F32)

    @pl.when(grp == 0)
    def _():
        xbuf[0:2] = jnp.zeros((2, R, 8, 256), BF16)

    @pl.when(grp == n_groups - 1)
    def _():
        xbuf[G + 2 : G + 4] = jnp.zeros((2, R, 8, 256), BF16)

    for c in loads:
        c.wait()

    def first_body(c, carry):
        e = 2 + 5 * c
        outs = transport([ext[e + i] for i in range(7)], {})
        for i in range(5):
            adv[e + i] = outs[i]
            packed[e + i] = outs[i].astype(BF16)
        return carry

    lax.fori_loop(0, 6, first_body, 0)

    expected = (
        (G - 1)
        + jnp.where(at_south, 0, 1)
        + jnp.where(at_north, 0, 1)
        + jnp.where(has_other, G, 0)
    )
    pl.semaphore_wait(barrier, expected)

    to_north = pltpu.make_async_remote_copy(
        ext.at[pl.ds(32, 2)], ext.at[pl.ds(0, 2)], halo_send.at[0], halo_recv.at[0],
        device_id=(lat + 1, wide), device_id_type=MESH,
    )
    to_south = pltpu.make_async_remote_copy(
        ext.at[pl.ds(2, 2)], ext.at[pl.ds(34, 2)], halo_send.at[1], halo_recv.at[1],
        device_id=(lat - 1, wide), device_id_type=MESH,
    )

    @pl.when(jnp.logical_not(at_north))
    def _():
        to_north.start()

    @pl.when(jnp.logical_not(at_south))
    def _():
        to_south.start()

    def local_row(k, c):
        return (NCH - 1 - c) * CH if k == 0 else c * CH

    def x_copy(k, c, group, slab, sem):
        row = local_row(k, c)
        return pltpu.make_async_remote_copy(
            packed.at[pl.ds(STARTS[k] + row, CH)],
            xbuf.at[slab, pl.ds(row, CH)],
            x_send.at[sem, k, c],
            x_recv.at[slab, c],
            device_id=(lat, group * G + k),
            device_id_type=MESH,
        )

    def each_x(k, c, act_on):
        @pl.when(has_other)
        def _():
            act_on(x_copy(k, c, og, os, 1))

        @pl.when(m != k)
        def _():
            act_on(x_copy(k, c, grp, m + 2, 0))

    for c in range(NCH):
        for k in range(G):
            if c < NCH - 1 or k in (1, 2):
                each_x(k, c, lambda d: d.start())

    @pl.when(jnp.logical_not(at_south))
    def _():
        to_north.wait_recv()

    @pl.when(jnp.logical_not(at_north))
    def _():
        to_south.wait_recv()

    south_open = jnp.where(at_south, 0.0, 1.0).astype(F32)
    north_open = jnp.where(at_north, 0.0, 1.0).astype(F32)
    for e, mask in ((0, south_open), (32, north_open)):
        outs = transport([ext[e + i] for i in range(4)], {1: mask})
        for i in range(2):
            adv[e + i] = outs[i]
            packed[e + i] = outs[i].astype(BF16)
    for k in (0, 3):
        each_x(k, NCH - 1, lambda d: d.start())

    mine = (25 * m + 1) // 3
    xbuf[pl.ds(m + 2, 1)] = packed[pl.ds(mine, R)][None]

    def iota(shape, d):
        return lax.broadcasted_iota(jnp.int32, shape, d)

    def one(cond):
        return jnp.where(cond, 1.0, 0.0)

    eye = one(iota((64, 64), 0) == iota((64, 64), 1)).astype(BF16)

    def transposed(w):
        return lax.dot_general(eye, w, (((1,), (1,)), ((), ())), preferred_element_type=F32)

    stage[...] = jnp.zeros((24, 64), F32)
    for k in range(3):
        stage[8 * k : 8 * k + 4] = w1_ref[k].astype(F32)
    w1t = (0.5 * transposed(stage[...].astype(BF16))).astype(BF16)
    row = iota((24, 64), 0)
    col = iota((24, 64), 1)
    same_field = (row & 7) == ((col & 7) >> 1)
    level_in = 2 * (col >> 3) + (col & 1)
    for j in range(14):
        band = one(jnp.logical_and(same_field, level_in == j + (row >> 3))).astype(BF16)
        level = 2 * G * grp + j - 3
        valid = jnp.where(
            jnp.logical_and(level >= 0, level < 2 * G * n_groups), 1.0, 0.0
        ).astype(F32)
        wa[64 * j : 64 * j + 64] = (dot(w1t, band) * valid).astype(BF16)
    zeros = jnp.zeros((64, 64), F32)
    for w_ref, band_ref in ((w2_ref, wb2), (w3_ref, wb3)):
        taps = [0.5 * transposed(w_ref[k]) for k in range(3)]
        for o in range(6):
            off = o - 2
            parts = [taps[i - off] if 0 <= i - off < 3 else zeros for i in range(4)]
            band_ref[64 * o : 64 * o + 64] = jnp.concatenate(parts, axis=1).astype(BF16)
    rho = iota((32, 64), 0)
    level_out = 2 * (rho >> 3) + (rho & 1)
    stage[0:8] = jnp.zeros((8, 64), F32)
    pick = one(iota((32, 8), 1) == ((iota((32, 8), 0) & 7) >> 1)).astype(BF16)
    last = []
    for k in range(3):
        stage[0:4] = w4_ref[k].astype(F32)
        last.append(dot(pick, stage[0:8].astype(BF16)))
    for t in range(3):
        parts = []
        for i in range(4):
            part = jnp.zeros((32, 64), F32)
            for k in range(3):
                part = part + jnp.where(level_out == 4 * t + i - k, last[k], 0.0)
            parts.append(part)
        wd[t] = jnp.concatenate(parts, axis=1).astype(BF16)

    low_valid = jnp.where(grp == 0, 0.0, 1.0).astype(F32)
    high_valid = jnp.where(grp == n_groups - 1, 0.0, 1.0).astype(F32)

    def one_row(r):
        x = jnp.concatenate([xbuf[s, r].astype(F32) for s in range(SLABS)], axis=0).astype(BF16)
        for q in range(7):
            h1[128 * q : 128 * q + 128] = act(dot(wa[128 * q : 128 * q + 128], x)).astype(BF16)
        y0 = dot(wb2[128:384], h1[0:256])
        y1 = dot(wb2[...], h1[256:512])
        y2 = dot(wb2[...], h1[512:768])
        y3 = dot(wb2[0:128, 0:128], h1[768:896])
        z = (
            y0[0:128] * low_valid, y0[128:256] + y1[0:128], y1[128:256],
            y1[256:384] + y2[0:128], y2[128:256], (y2[256:384] + y3) * high_valid,
        )
        for p in range(6):
            held = h1[64 + 128 * p : 192 + 128 * p].astype(F32)
            h2[128 * p : 128 * p + 128] = (held + act(z[p])).astype(BF16)
        y0 = dot(wb3[128:384], h2[0:256])
        y1 = dot(wb3[...], h2[256:512])
        y2 = dot(wb3[0:256], h2[512:768])
        z = (
            y0[0:64] * low_valid, y0[64:128], y0[128:256] + y1[0:128], y1[128:256],
            y1[256:384] + y2[0:128], y2[128:192], y2[192:256] * high_valid,
        )
        at = 0
        for v in z:
            size = v.shape[0]
            held = h2[64 + at : 64 + at + size].astype(F32)
            h3[at : at + size] = (held + act(v)).astype(BF16)
            at += size
        out = dot(wd[0], h3[0:256]) + dot(wd[1], h3[256:512]) + dot(wd[2][:, 0:128], h3[512:640])
        for k in range(G):
            tsend[k, r] = out[8 * k : 8 * k + 8].astype(BF16)

    def base_of(c):
        return jnp.where(m == 0, (NCH - 1 - c) * CH, c * CH)

    def t_copy(k, c):
        return pltpu.make_async_remote_copy(
            tsend.at[k, pl.ds(base_of(c), CH)],
            tin.at[m, pl.ds(base_of(c), CH)],
            t_send.at[k, c],
            t_recv.at[m, c],
            device_id=(lat, grp * G + k),
            device_id_type=MESH,
        )

    def x_arrived(s, c):
        d = pltpu.make_async_remote_copy(
            packed.at[pl.ds(0, CH)], xbuf.at[s, pl.ds(base_of(c), CH)],
            x_send.at[0, 0, c], x_recv.at[s, c], device_id=(lat, wide), device_id_type=MESH,
        )
        d.wait_recv()

    for c in range(NCH):
        for s in range(SLABS):
            if s < 2:
                cond = grp > 0
            elif s >= G + 2:
                cond = grp < n_groups - 1
            else:
                cond = m != s - 2

            @pl.when(cond)
            def _():
                x_arrived(s, c)

        def row_body(i, carry):
            one_row(base_of(c) + i)
            return carry

        lax.fori_loop(0, CH, row_body, 0)
        for k in range(G):
            @pl.when(m != k)
            def _():
                t_copy(k, c).start()

    tin[pl.ds(m, 1)] = tsend[pl.ds(m, 1)]

    for k in range(G):
        @pl.when(m != k)
        def _():
            for c in range(NCH):
                d = pltpu.make_async_remote_copy(
                    tsend.at[k, pl.ds(local_row(k, c), CH)],
                    tin.at[k, pl.ds(local_row(k, c), CH)],
                    t_send.at[k, c], t_recv.at[k, c],
                    device_id=(lat, wide), device_id_type=MESH,
                )
                d.wait_recv()

        first = STARTS[k] if k == 0 else STARTS[k - 1] + R
        for e in range(first, STARTS[k] + R):
            adv[e] = adv[e] + tin[k, e - STARTS[k]].astype(F32)

    def second_body(c, carry):
        e = 4 * c
        low = jnp.where(jnp.logical_and(at_south, c == 0), 0.0, 1.0).astype(F32)
        high = jnp.where(jnp.logical_and(at_north, c == 7), 0.0, 1.0).astype(F32)
        outs = transport([adv[e + i] for i in range(6)], {0: low, 4: high})
        for i in range(4):
            outv[e + i] = outs[i]
        return carry

    lax.fori_loop(0, 8, second_body, 0)
    stores = []
    for f in range(4):
        for l in range(2):
            stores.append(
                pltpu.make_async_copy(
                    outv.at[:, 2 * f + l], out_ref.at[f, l], in_sem.at[2 * f + l]
                )
            )
    for c in stores:
        c.start()

    @pl.when(jnp.logical_not(at_north))
    def _():
        to_north.wait_send()

    @pl.when(jnp.logical_not(at_south))
    def _():
        to_south.wait_send()

    for c in range(NCH):
        for k in range(G):
            each_x(k, c, lambda d: d.wait_send())

            @pl.when(m != k)
            def _():
                t_copy(k, c).wait_send()

    for c in stores:
        c.wait()


def on_device(fields, w_first, w_second, w_third, w_last):
    vmem = pl.BlockSpec(memory_space=pltpu.VMEM)
    return pl.pallas_call(
        kernel,
        out_shape=jax.ShapeDtypeStruct(fields.shape, F32),
        in_specs=[pl.BlockSpec(memory_space=pl.ANY), vmem, vmem, vmem, vmem],
        out_specs=pl.BlockSpec(memory_space=pl.ANY),
        scratch_shapes=[
            pltpu.VMEM((36, 8, 256), F32),
            pltpu.VMEM((34, 8, 256), F32),
            pltpu.VMEM((34, 8, 256), BF16),
            pltpu.VMEM((SLABS, R, 8, 256), BF16),
            pltpu.VMEM((G, R, 8, 256), BF16),
            pltpu.VMEM((G, R, 8, 256), BF16),
            pltpu.VMEM((32, 8, 256), F32),
            pltpu.VMEM((14 * 64, 64), BF16),
            pltpu.VMEM((6 * 64, 256), BF16),
            pltpu.VMEM((6 * 64, 256), BF16),
            pltpu.VMEM((3, 32, 256), BF16),
            pltpu.VMEM((24, 64), F32),
            pltpu.VMEM((14 * 64, 256), BF16),
            pltpu.VMEM((12 * 64, 256), BF16),
            pltpu.VMEM((10 * 64, 256), BF16),
            pltpu.SemaphoreType.DMA((8,)),
            pltpu.SemaphoreType.DMA((2,)),
            pltpu.SemaphoreType.DMA((2,)),
            pltpu.SemaphoreType.DMA((2, G, NCH)),
            pltpu.SemaphoreType.DMA((SLABS, NCH)),
            pltpu.SemaphoreType.DMA((G, NCH)),
            pltpu.SemaphoreType.DMA((G, NCH)),
        ],
        compiler_params=pltpu.CompilerParams(collective_id=0, has_side_effects=True),
        name="climate_step",
    )(fields, w_first, w_second, w_third, jnp.transpose(w_last, (0, 2, 1)))


def solution(mesh):
    return jax.shard_map(
        on_device,
        mesh=mesh,
        in_specs=(P(None, "wide", "lat", None), P(), P(), P(), P()),
        out_specs=P(None, "wide", "lat", None),
        check_vma=False,
    )
```

time: 86 us -> 30.9 us (0.36)
  the two profiles are of different devices: /device:TPU:1 before, /device:TPU:6 now
where the time goes in v1:
time: 30.9 us; the launch traced here: 30.6 us
  Pallas kernels  29 us (94%)
  local copies, waits for them, and re-layouts  1.67 us (5%)
    pallas_call x1, Pallas kernels, on_device(): pl.pallas_call(kernel, out_shape=jax.ShapeDtypeStruct(fields.shape, F32),...  29 us
    unnamed x1, local copies, waits for them, and re-layouts  1.67 us

profile of v1, /device:TPU:6, one launch (start us, length us, event | category | flops | bytes accessed | tf_op | source)
XLA Modules:
  0.0 30.6 jit_solution(17417817422757777374)
XLA Ops:
  0.0 29.0 %climate_step.1 = f32[4,2,32,256]{3,2,1,0:T(8,128)} custom-call(f32[4,2,32,256]{3,2,1,0:T(8,128)} %f_hbm.1, bf16[3,4,64]{2,1,0:T(4,128)(2,1)} %w1_ref.1, bf16[3,64,64]{2,1,0:T(8,128)(2,1)} %w2_ref.1, bf16[3,64,64]{2,1,0:T(8,128)(2,1)} %w3_ref.1, bf16[3,4,64]{2,1,0:T(4,128)(2,1)} %bitcast.1), custom_call_target="tpu_custom_call" | custom-call | tf_op jit(solution)/shard_map/climate_step/pallas_call | solution.py:414
  29.0 1.7 %copy.7 = f32[4,2,32,256]{3,2,1,0:T(8,128)} copy(f32[4,2,32,256]{3,2,1,0:T(8,128)} %climate_step.1) | data formatting | bytes 524288

commit v2 on v1

--- a/solution.py
+++ b/solution.py
@@ -17,8 +17,10 @@
 SLABS = G + 4
 
 
-def smooth_abs(v):
-    return jnp.sqrt(v * v + 0.01)
+def face_terms(total):
+    face = 0.075 * total
+    square = face * face + 0.15 * 0.15 * 0.01
+    return face, square * lax.rsqrt(square)
 
 
 def spread(v, first):
@@ -36,8 +38,8 @@
     fluxes = []
     for j in range(n + 1):
         low, high = rows[j], rows[j + 1]
-        face = 0.5 * (winds[j] + winds[j + 1])
-        flux = 0.5 * face * (low + high) - 0.5 * smooth_abs(face) * (high - low)
+        face, speed = face_terms(winds[j] + winds[j + 1])
+        flux = face * (low + high) - speed * (high - low)
         if j in masks:
             flux = flux * masks[j]
         fluxes.append(flux)
@@ -46,11 +48,11 @@
         cell = rows[j + 1]
         lanes = cell.shape[1]
         wind = spread(cell, 0)
-        face = 0.5 * (wind + pltpu.roll(wind, lanes - 1, 1))
+        face, speed = face_terms(wind + pltpu.roll(wind, lanes - 1, 1))
         after = pltpu.roll(cell, lanes - 1, 1)
-        flux = 0.5 * face * (cell + after) - 0.5 * smooth_abs(face) * (after - cell)
+        flux = face * (cell + after) - speed * (after - cell)
         div = flux - pltpu.roll(flux, 1, 1)
-        outs.append(cell - 0.3 * (div + (fluxes[j + 1] - fluxes[j])))
+        outs.append(cell - (div + (fluxes[j + 1] - fluxes[j])))
     return outs
 
 
@@ -63,9 +65,10 @@
 
 
 def kernel(
-    f_hbm, w1_ref, w2_ref, w3_ref, w4_ref, out_ref,
-    ext, adv, packed, xbuf, tsend, tin, outv, wa, wb2, wb3, wd, stage, h1, h2, h3,
-    in_sem, halo_send, halo_recv, x_send, x_recv, t_send, t_recv,
+    f_hbm, w1_hbm, w2_hbm, w3_hbm, w4_hbm, upd_ref,
+    ext, adv, packed, xbuf, tsend, tin, w1_ref, w2_ref, w3_ref, w4_ref,
+    wa, wb, band2, band3, wd, stage, h1, h2, h3,
+    in_sem, w_sem, halo_send, halo_recv, x_send, x_recv, t_send, t_recv,
 ):
     lat = lax.axis_index("lat")
     wide = lax.axis_index("wide")
@@ -118,6 +121,14 @@
             )
     for c in loads:
         c.start()
+    w_loads = [
+        pltpu.make_async_copy(src, dst, w_sem.at[k])
+        for k, (src, dst) in enumerate(
+            ((w1_hbm, w1_ref), (w2_hbm, w2_ref), (w3_hbm, w3_ref), (w4_hbm, w4_ref))
+        )
+    ]
+    for c in w_loads:
+        c.start()
 
     @pl.when(at_south)
     def _():
@@ -222,6 +233,9 @@
     mine = (25 * m + 1) // 3
     xbuf[pl.ds(m + 2, 1)] = packed[pl.ds(mine, R)][None]
 
+    for c in w_loads:
+        c.wait()
+
     def iota(shape, d):
         return lax.broadcasted_iota(jnp.int32, shape, d)
 
@@ -237,36 +251,42 @@
     for k in range(3):
         stage[8 * k : 8 * k + 4] = w1_ref[k].astype(F32)
     w1t = (0.5 * transposed(stage[...].astype(BF16))).astype(BF16)
-    row = iota((24, 64), 0)
-    col = iota((24, 64), 1)
-    same_field = (row & 7) == ((col & 7) >> 1)
-    level_in = 2 * (col >> 3) + (col & 1)
-    for j in range(14):
+
+    def first_band(j, slab, width):
+        row = iota((24, width), 0)
+        col = iota((24, width), 1)
+        same_field = (row & 7) == ((col & 7) >> 1)
+        level_in = 2 * (slab + (col >> 3)) + (col & 1)
         band = one(jnp.logical_and(same_field, level_in == j + (row >> 3))).astype(BF16)
         level = 2 * G * grp + j - 3
         valid = jnp.where(
             jnp.logical_and(level >= 0, level < 2 * G * n_groups), 1.0, 0.0
         ).astype(F32)
-        wa[64 * j : 64 * j + 64] = (dot(w1t, band) * valid).astype(BF16)
+        return (dot(w1t, band) * valid).astype(BF16)
+
+    for j in range(4, 14):
+        wa[64 * (j - 4) : 64 * (j - 3)] = first_band(j, 2, 48)
+    for j in range(4):
+        wb[64 * j : 64 * j + 64] = first_band(j, 0, 32)
     zeros = jnp.zeros((64, 64), F32)
-    for w_ref, band_ref in ((w2_ref, wb2), (w3_ref, wb3)):
+    for w_ref, band_ref in ((w2_ref, band2), (w3_ref, band3)):
         taps = [0.5 * transposed(w_ref[k]) for k in range(3)]
         for o in range(6):
             off = o - 2
             parts = [taps[i - off] if 0 <= i - off < 3 else zeros for i in range(4)]
             band_ref[64 * o : 64 * o + 64] = jnp.concatenate(parts, axis=1).astype(BF16)
-    rho = iota((32, 64), 0)
+    rho = iota((16, 64), 0)
     level_out = 2 * (rho >> 3) + (rho & 1)
     stage[0:8] = jnp.zeros((8, 64), F32)
-    pick = one(iota((32, 8), 1) == ((iota((32, 8), 0) & 7) >> 1)).astype(BF16)
+    pick = one(iota((16, 8), 1) == ((iota((16, 8), 0) & 7) >> 1)).astype(BF16)
     last = []
     for k in range(3):
         stage[0:4] = w4_ref[k].astype(F32)
         last.append(dot(pick, stage[0:8].astype(BF16)))
-    for t in range(3):
+    for t in range(2):
         parts = []
         for i in range(4):
-            part = jnp.zeros((32, 64), F32)
+            part = jnp.zeros((16, 64), F32)
             for k in range(3):
                 part = part + jnp.where(level_out == 4 * t + i - k, last[k], 0.0)
             parts.append(part)
@@ -274,38 +294,6 @@
 
     low_valid = jnp.where(grp == 0, 0.0, 1.0).astype(F32)
     high_valid = jnp.where(grp == n_groups - 1, 0.0, 1.0).astype(F32)
-
-    def one_row(r):
-        x = jnp.concatenate([xbuf[s, r].astype(F32) for s in range(SLABS)], axis=0).astype(BF16)
-        for q in range(7):
-            h1[128 * q : 128 * q + 128] = act(dot(wa[128 * q : 128 * q + 128], x)).astype(BF16)
-        y0 = dot(wb2[128:384], h1[0:256])
-        y1 = dot(wb2[...], h1[256:512])
-        y2 = dot(wb2[...], h1[512:768])
-        y3 = dot(wb2[0:128, 0:128], h1[768:896])
-        z = (
-            y0[0:128] * low_valid, y0[128:256] + y1[0:128], y1[128:256],
-            y1[256:384] + y2[0:128], y2[128:256], (y2[256:384] + y3) * high_valid,
-        )
-        for p in range(6):
-            held = h1[64 + 128 * p : 192 + 128 * p].astype(F32)
-            h2[128 * p : 128 * p + 128] = (held + act(z[p])).astype(BF16)
-        y0 = dot(wb3[128:384], h2[0:256])
-        y1 = dot(wb3[...], h2[256:512])
-        y2 = dot(wb3[0:256], h2[512:768])
-        z = (
-            y0[0:64] * low_valid, y0[64:128], y0[128:256] + y1[0:128], y1[128:256],
-            y1[256:384] + y2[0:128], y2[128:192], y2[192:256] * high_valid,
-        )
-        at = 0
-        for v in z:
-            size = v.shape[0]
-            held = h2[64 + at : 64 + at + size].astype(F32)
-            h3[at : at + size] = (held + act(v)).astype(BF16)
-            at += size
-        out = dot(wd[0], h3[0:256]) + dot(wd[1], h3[256:512]) + dot(wd[2][:, 0:128], h3[512:640])
-        for k in range(G):
-            tsend[k, r] = out[8 * k : 8 * k + 8].astype(BF16)
 
     def base_of(c):
         return jnp.where(m == 0, (NCH - 1 - c) * CH, c * CH)
@@ -321,73 +309,114 @@
         )
 
     def x_arrived(s, c):
-        d = pltpu.make_async_remote_copy(
+        pltpu.make_async_remote_copy(
             packed.at[pl.ds(0, CH)], xbuf.at[s, pl.ds(base_of(c), CH)],
             x_send.at[0, 0, c], x_recv.at[s, c], device_id=(lat, wide), device_id_type=MESH,
-        )
-        d.wait_recv()
-
-    for c in range(NCH):
-        for s in range(SLABS):
-            if s < 2:
-                cond = grp > 0
-            elif s >= G + 2:
-                cond = grp < n_groups - 1
-            else:
-                cond = m != s - 2
+        ).wait_recv()
+
+    def columns_of(r, first, last):
+        parts = [xbuf[s, r].astype(F32) for s in range(first, last)]
+        return jnp.concatenate(parts, axis=0).astype(BF16)
+
+    def store_sum(dst, src, r, at, z):
+        held = src[r, at + 64 : at + 64 + z.shape[0]].astype(F32)
+        dst[r, at : at + z.shape[0]] = (held + act(z)).astype(BF16)
+
+    def upper(c, carry):
+        for s in range(2, SLABS):
+            cond = grp < n_groups - 1 if s >= G + 2 else m != s - 2
 
             @pl.when(cond)
             def _():
                 x_arrived(s, c)
 
-        def row_body(i, carry):
-            one_row(base_of(c) + i)
-            return carry
-
-        lax.fori_loop(0, CH, row_body, 0)
-        for k in range(G):
+        rows = [base_of(c) + i for i in range(CH)]
+        for r in rows:
+            x = columns_of(r, 2, SLABS)
+            for q in range(5):
+                h1[r, 256 + 128 * q : 384 + 128 * q] = act(
+                    dot(wa[128 * q : 128 * q + 128], x)
+                ).astype(BF16)
+        for r in rows:
+            y1 = dot(band2[128:384], h1[r, 256:512])
+            y2 = dot(band2[...], h1[r, 512:768])
+            y3 = dot(band2[0:128, 0:128], h1[r, 768:896])
+            store_sum(h2, h1, r, 256, y1[0:128])
+            store_sum(h2, h1, r, 384, y1[128:256] + y2[0:128])
+            store_sum(h2, h1, r, 512, y2[128:256])
+            store_sum(h2, h1, r, 640, (y2[256:384] + y3) * high_valid)
+        for r in rows:
+            y1 = dot(band3[128:384], h2[r, 256:512])
+            y2 = dot(band3[0:256], h2[r, 512:768])
+            store_sum(h3, h2, r, 256, y1[0:128])
+            store_sum(h3, h2, r, 384, y1[128:256] + y2[0:128])
+            store_sum(h3, h2, r, 512, y2[128:192])
+            store_sum(h3, h2, r, 576, y2[192:256] * high_valid)
+        for r in rows:
+            out = dot(wd[0], h3[r, 256:512]) + dot(wd[1][:, 0:128], h3[r, 512:640])
+            for k in (2, 3):
+                tsend[k, r] = out[8 * (k - 2) : 8 * (k - 1)].astype(BF16)
+        for k in (2, 3):
             @pl.when(m != k)
             def _():
                 t_copy(k, c).start()
 
+        return carry
+
+    lax.fori_loop(0, NCH, upper, 0)
+
+    def lower(c, carry):
+        for s in (0, 1):
+            @pl.when(grp > 0)
+            def _():
+                x_arrived(s, c)
+
+        rows = [base_of(c) + i for i in range(CH)]
+        for r in rows:
+            x = columns_of(r, 0, 4)
+            for q in range(2):
+                h1[r, 128 * q : 128 * q + 128] = act(
+                    dot(wb[128 * q : 128 * q + 128], x)
+                ).astype(BF16)
+        for r in rows:
+            y0 = dot(band2[128:384], h1[r, 0:256])
+            y1 = dot(band2[0:128, 0:128], h1[r, 256:384])
+            store_sum(h2, h1, r, 0, y0[0:128] * low_valid)
+            store_sum(h2, h1, r, 128, y0[128:256] + y1)
+        for r in rows:
+            y0 = dot(band3[128:384], h2[r, 0:256])
+            y1 = dot(band3[0:128, 0:128], h2[r, 256:384])
+            store_sum(h3, h2, r, 0, y0[0:64] * low_valid)
+            store_sum(h3, h2, r, 64, y0[64:128])
+            store_sum(h3, h2, r, 128, y0[128:256] + y1)
+        for r in rows:
+            out = dot(wd[0], h3[r, 0:256]) + dot(wd[1][:, 0:128], h3[r, 256:384])
+            for k in (0, 1):
+                tsend[k, r] = out[8 * k : 8 * k + 8].astype(BF16)
+        for k in (0, 1):
+            @pl.when(m != k)
+            def _():
+                t_copy(k, c).start()
+
+        return carry
+
+    lax.fori_loop(0, NCH, lower, 0)
     tin[pl.ds(m, 1)] = tsend[pl.ds(m, 1)]
 
     for k in range(G):
         @pl.when(m != k)
         def _():
             for c in range(NCH):
-                d = pltpu.make_async_remote_copy(
+                pltpu.make_async_remote_copy(
                     tsend.at[k, pl.ds(local_row(k, c), CH)],
                     tin.at[k, pl.ds(local_row(k, c), CH)],
                     t_send.at[k, c], t_recv.at[k, c],
                     device_id=(lat, wide), device_id_type=MESH,
-                )
-                d.wait_recv()
+                ).wait_recv()
 
         first = STARTS[k] if k == 0 else STARTS[k - 1] + R
         for e in range(first, STARTS[k] + R):
-            adv[e] = adv[e] + tin[k, e - STARTS[k]].astype(F32)
-
-    def second_body(c, carry):
-        e = 4 * c
-        low = jnp.where(jnp.logical_and(at_south, c == 0), 0.0, 1.0).astype(F32)
-        high = jnp.where(jnp.logical_and(at_north, c == 7), 0.0, 1.0).astype(F32)
-        outs = transport([adv[e + i] for i in range(6)], {0: low, 4: high})
-        for i in range(4):
-            outv[e + i] = outs[i]
-        return carry
-
-    lax.fori_loop(0, 8, second_body, 0)
-    stores = []
-    for f in range(4):
-        for l in range(2):
-            stores.append(
-                pltpu.make_async_copy(
-                    outv.at[:, 2 * f + l], out_ref.at[f, l], in_sem.at[2 * f + l]
-                )
-            )
-    for c in stores:
-        c.start()
+            upd_ref[e] = adv[e] + tin[k, e - STARTS[k]].astype(F32)
 
     @pl.when(jnp.logical_not(at_north))
     def _():
@@ -405,17 +434,44 @@
             def _():
                 t_copy(k, c).wait_send()
 
-    for c in stores:
-        c.wait()
+
+def second_kernel(upd_ref, out_ref, outv, sem):
+    lat = lax.axis_index("lat")
+    at_south = lat == 0
+    at_north = lat == lax.axis_size("lat") - 1
+    stores = []
+    for c in range(4):
+        masks = {}
+        if c == 0:
+            masks = {0: jnp.where(at_south, 0.0, 1.0).astype(F32)}
+        if c == 3:
+            masks = {8: jnp.where(at_north, 0.0, 1.0).astype(F32)}
+        e = 8 * c
+        outs = transport([upd_ref[e + i] for i in range(10)], masks)
+        for i in range(8):
+            outv[e + i] = outs[i]
+        for f in range(4):
+            for l in range(2):
+                d = pltpu.make_async_copy(
+                    outv.at[pl.ds(e, 8), 2 * f + l],
+                    out_ref.at[f, l, pl.ds(e, 8)],
+                    sem.at[c, 2 * f + l],
+                )
+                d.start()
+                stores.append(d)
+    for d in stores:
+        d.wait()
 
 
 def on_device(fields, w_first, w_second, w_third, w_last):
+    anywhere = pl.BlockSpec(memory_space=pltpu.HBM)
     vmem = pl.BlockSpec(memory_space=pltpu.VMEM)
-    return pl.pallas_call(
+    dma = pltpu.SemaphoreType.DMA
+    updated = pl.pallas_call(
         kernel,
-        out_shape=jax.ShapeDtypeStruct(fields.shape, F32),
-        in_specs=[pl.BlockSpec(memory_space=pl.ANY), vmem, vmem, vmem, vmem],
-        out_specs=pl.BlockSpec(memory_space=pl.ANY),
+        out_shape=jax.ShapeDtypeStruct((34, 8, 256), F32),
+        in_specs=[anywhere] * 5,
+        out_specs=vmem,
         scratch_shapes=[
             pltpu.VMEM((36, 8, 256), F32),
             pltpu.VMEM((34, 8, 256), F32),
@@ -423,26 +479,42 @@
             pltpu.VMEM((SLABS, R, 8, 256), BF16),
             pltpu.VMEM((G, R, 8, 256), BF16),
             pltpu.VMEM((G, R, 8, 256), BF16),
-            pltpu.VMEM((32, 8, 256), F32),
-            pltpu.VMEM((14 * 64, 64), BF16),
+            pltpu.VMEM((3, 4, 64), BF16),
+            pltpu.VMEM((3, 64, 64), BF16),
+            pltpu.VMEM((3, 64, 64), BF16),
+            pltpu.VMEM((3, 4, 64), BF16),
+            pltpu.VMEM((10 * 64, 48), BF16),
+            pltpu.VMEM((4 * 64, 32), BF16),
             pltpu.VMEM((6 * 64, 256), BF16),
             pltpu.VMEM((6 * 64, 256), BF16),
-            pltpu.VMEM((3, 32, 256), BF16),
+            pltpu.VMEM((2, 16, 256), BF16),
             pltpu.VMEM((24, 64), F32),
-            pltpu.VMEM((14 * 64, 256), BF16),
-            pltpu.VMEM((12 * 64, 256), BF16),
-            pltpu.VMEM((10 * 64, 256), BF16),
-            pltpu.SemaphoreType.DMA((8,)),
-            pltpu.SemaphoreType.DMA((2,)),
-            pltpu.SemaphoreType.DMA((2,)),
-            pltpu.SemaphoreType.DMA((2, G, NCH)),
-            pltpu.SemaphoreType.DMA((SLABS, NCH)),
-            pltpu.SemaphoreType.DMA((G, NCH)),
-            pltpu.SemaphoreType.DMA((G, NCH)),
+            pltpu.VMEM((R, 14 * 64, 256), BF16),
+            pltpu.VMEM((R, 12 * 64, 256), BF16),
+            pltpu.VMEM((R, 10 * 64, 256), BF16),
+            dma((8,)),
+            dma((4,)),
+            dma((2,)),
+            dma((2,)),
+            dma((2, G, NCH)),
+            dma((SLABS, NCH)),
+            dma((G, NCH)),
+            dma((G, NCH)),
         ],
-        compiler_params=pltpu.CompilerParams(collective_id=0, has_side_effects=True),
+        compiler_params=pltpu.CompilerParams(
+            collective_id=0, has_side_effects=True, vmem_limit_bytes=32 * 1024 * 1024
+        ),
         name="climate_step",
-    )(fields, w_first, w_second, w_third, jnp.transpose(w_last, (0, 2, 1)))
+        )(*[pltpu.with_memory_space_constraint(v, pltpu.HBM) for v in (fields, w_first, w_second, w_third, jnp.transpose(w_last, (0, 2, 1)))])
+    return pl.pallas_call(
+        second_kernel,
+        out_shape=jax.ShapeDtypeStruct(fields.shape, F32),
+        in_specs=[vmem],
+        out_specs=anywhere,
+        scratch_shapes=[pltpu.VMEM((32, 8, 256), F32), dma((4, 8))],
+        compiler_params=pltpu.CompilerParams(vmem_limit_bytes=8 * 1024 * 1024),
+        name="climate_end",
+    )(updated)
 
 
 def solution(mesh):

time: 30.9 us -> 25.5 us (0.83)
  Pallas kernels: 29 us -> 25.4 us
  local copies, waits for them, and re-layouts: 1.67 us -> 0 us
    pallas_call x1 -> x2, Pallas kernels: 29 us -> 25.4 us  [the longest x1 23.7 us: on_device(): pl.pallas_call(kernel, out_shape=jax.ShapeDtypeStruct((34, 8, 256), F32),...]
    unnamed x1 -> x0, local copies, waits for them, and re-layouts: 1.67 us -> none
where the time goes in v2:
time: 25.5 us; the launch traced here: 25.4 us
  Pallas kernels  25.4 us (100%)
    pallas_call x1, Pallas kernels, on_device(): pl.pallas_call(kernel, out_shape=jax.ShapeDtypeStruct((34, 8, 256), F32),...  23.7 us
    pallas_call x1, Pallas kernels, on_device(): pl.pallas_call(second_kernel, out_shape=jax.ShapeDtypeStruct(fields.shape...  1.71 us

profile of v2, /device:TPU:6, one launch (start us, length us, event | category | flops | bytes accessed | tf_op | source)
XLA Modules:
  0.0 25.4 jit_solution(7554280572234178610)
XLA Ops:
  0.0 23.7 %climate_step.1.upd_ref = f32[34,8,256]{2,1,0:T(8,128)S(1)} custom-call(f32[4,2,32,256]{3,2,1,0:T(8,128)} %f_hbm.1, bf16[3,4,64]{2,1,0:T(4,128)(2,1)} %w1_hbm.1, bf16[3,64,64]{2,1,0:T(8,128)(2,1)} %w2_hbm.1, bf16[3,64,64]{2,1,0:T(8,128)(2,1)} %w3_hbm.1, bf16[3,4,64]{2,1,0:T(4,128)(2,1)} %bitcast.1), custom_call_target="tpu_custom_call" | custom-call | tf_op jit(solution)/shard_map/climate_step/pallas_call | solution.py:470
  23.7 1.7 %climate_end.1 = f32[4,2,32,256]{3,2,1,0:T(8,128)} custom-call(f32[34,8,256]{2,1,0:T(8,128)S(1)} %climate_step.1.upd_ref), custom_call_target="tpu_custom_call" | custom-call | tf_op jit(solution)/shard_map/climate_end/pallas_call | solution.py:509

commit v3 on v2

v3 whole, which is shorter than its diff:
```python
import jax
import jax.numpy as jnp
from jax import lax
from jax.experimental import pallas as pl
from jax.experimental.pallas import tpu as pltpu
from jax.sharding import PartitionSpec as P

MESH = pl.DeviceIdType.MESH
F32 = jnp.float32
BF16 = jnp.bfloat16

G = 4
R = 9
STARTS = (0, 8, 17, 25)
CH = 3
NCH = R // CH
SLABS = G + 4
UPPER = ((0,), (1,), (2,))
LOWER = ((0,), (1,), (2,))


def face_terms(total):
    face = 0.075 * total
    square = face * face + 0.15 * 0.15 * 0.01
    return face, square * lax.rsqrt(square)


def spread(v, first):
    sub = lax.broadcasted_iota(jnp.int32, v.shape, 0)
    if first == 0:
        pair = jnp.where(sub < 2, v, pltpu.roll(v, 2, 0))
    else:
        pair = jnp.where(sub < 2, pltpu.roll(v, 6, 0), v)
    return jnp.where(sub < 4, pair, pltpu.roll(pair, 4, 0))


def transport(rows, masks):
    n = len(rows) - 2
    winds = [spread(v, 2) for v in rows]
    fluxes = []
    for j in range(n + 1):
        low, high = rows[j], rows[j + 1]
        face, speed = face_terms(winds[j] + winds[j + 1])
        flux = face * (low + high) - speed * (high - low)
        if j in masks:
            flux = flux * masks[j]
        fluxes.append(flux)
    outs = []
    for j in range(n):
        cell = rows[j + 1]
        lanes = cell.shape[1]
        wind = spread(cell, 0)
        face, speed = face_terms(wind + pltpu.roll(wind, lanes - 1, 1))
        after = pltpu.roll(cell, lanes - 1, 1)
        flux = face * (cell + after) - speed * (after - cell)
        div = flux - pltpu.roll(flux, 1, 1)
        outs.append(cell - (div + (fluxes[j + 1] - fluxes[j])))
    return outs


def act(t):
    return t + t * jnp.tanh(t)


def dot(a, b):
    return jnp.dot(a, b, preferred_element_type=F32)


def kernel(
    f_hbm, w1_hbm, w2_hbm, w3_hbm, w4_hbm, upd_ref,
    ext, adv, packed, xbuf, tsend, tin, w1_ref, w2_ref, w3_ref, w4_ref,
    band1, band2, band3, wd, stage, h1, h2, h3,
    in_sem, w_sem, halo_send, halo_recv, x_send, x_recv, f_send, f_recv, t_send, t_recv, ready,
):
    lat = lax.axis_index("lat")
    wide = lax.axis_index("wide")
    n_lat = lax.axis_size("lat")
    n_groups = lax.axis_size("wide") // G
    grp = wide // G
    m = wide % G
    at_south = lat == 0
    at_north = lat == n_lat - 1
    has_low = grp > 0
    has_high = grp < n_groups - 1

    barrier = pltpu.get_barrier_semaphore()

    def greet(la, wi):
        pl.semaphore_signal(barrier, inc=1, device_id=(la, wi), device_id_type=MESH)

    @pl.when(has_low)
    def _():
        greet(lat, wide - G)

    for k in range(G):
        @pl.when(m != k)
        def _():
            greet(lat, grp * G + k)

    @pl.when(jnp.logical_not(at_south))
    def _():
        greet(lat - 1, wide)

    @pl.when(jnp.logical_not(at_north))
    def _():
        greet(lat + 1, wide)

    loads = []
    for f in range(4):
        for l in range(2):
            loads.append(
                pltpu.make_async_copy(
                    f_hbm.at[f, l], ext.at[pl.ds(2, 32), 2 * f + l], in_sem.at[2 * f + l]
                )
            )
    for c in loads:
        c.start()
    w_loads = [
        pltpu.make_async_copy(src, dst, w_sem.at[k])
        for k, (src, dst) in enumerate(
            ((w1_hbm, w1_ref), (w2_hbm, w2_ref), (w3_hbm, w3_ref), (w4_hbm, w4_ref))
        )
    ]
    for c in w_loads:
        c.start()

    @pl.when(at_south)
    def _():
        ext[0:2] = jnp.zeros((2, 8, 256), F32)

    @pl.when(at_north)
    def _():
        ext[34:36] = jnp.zeros((2, 8, 256), F32)

    @pl.when(grp == 0)
    def _():
        xbuf[0:2] = jnp.zeros((2, R, 8, 256), BF16)

    @pl.when(grp == n_groups - 1)
    def _():
        xbuf[G + 2 : G + 4] = jnp.zeros((2, R, 8, 256), BF16)

    for c in loads:
        c.wait()

    def local_row(k, c):
        return (NCH - 1 - c) * CH if k == 0 else c * CH

    def base_of(c):
        return jnp.where(m == 0, (NCH - 1 - c) * CH, c * CH)

    def first_transport(k, c, masks):
        e = STARTS[k] + local_row(k, c)
        n = CH - 1 if (k, c) == (2, NCH - 1) else CH
        outs = transport([ext[e + i] for i in range(n + 2)], masks)
        for i in range(n):
            adv[e + i] = outs[i]
            packed[e + i] = outs[i].astype(BF16)

    def x_copy(k, c):
        row = local_row(k, c)
        return pltpu.make_async_remote_copy(
            packed.at[pl.ds(STARTS[k] + row, CH)],
            xbuf.at[m + 2, pl.ds(row, CH)],
            x_send.at[k, c],
            x_recv.at[m, c],
            device_id=(lat, grp * G + k),
            device_id_type=MESH,
        )

    def send_x(k, c):
        @pl.when(m != k)
        def _():
            x_copy(k, c).start()

    for k in range(G):
        first_transport(k, 0, {})

    expected = (
        (G - 1)
        + jnp.where(at_south, 0, 1)
        + jnp.where(at_north, 0, 1)
        + jnp.where(has_high, 1, 0)
    )
    pl.semaphore_wait(barrier, expected)

    @pl.when(has_high)
    def _():
        pl.semaphore_signal(ready, inc=1, device_id=(lat, wide + G), device_id_type=MESH)

    to_north = pltpu.make_async_remote_copy(
        ext.at[pl.ds(32, 2)], ext.at[pl.ds(0, 2)], halo_send.at[0], halo_recv.at[0],
        device_id=(lat + 1, wide), device_id_type=MESH,
    )
    to_south = pltpu.make_async_remote_copy(
        ext.at[pl.ds(2, 2)], ext.at[pl.ds(34, 2)], halo_send.at[1], halo_recv.at[1],
        device_id=(lat - 1, wide), device_id_type=MESH,
    )

    @pl.when(jnp.logical_not(at_north))
    def _():
        to_north.start()

    @pl.when(jnp.logical_not(at_south))
    def _():
        to_south.start()

    for k in range(G):
        send_x(k, 0)
    for k in range(G):
        first_transport(k, 1, {})
    for k in range(G):
        send_x(k, 1)
    for k in (1, 2):
        first_transport(k, NCH - 1, {})
    for k in (1, 2):
        send_x(k, NCH - 1)

    for c in w_loads:
        c.wait()

    def iota(shape, d):
        return lax.broadcasted_iota(jnp.int32, shape, d)

    def one(cond):
        return jnp.where(cond, 1.0, 0.0)

    eye = one(iota((64, 64), 0) == iota((64, 64), 1)).astype(BF16)

    def transposed(w):
        return lax.dot_general(eye, w, (((1,), (1,)), ((), ())), preferred_element_type=F32)

    stage[...] = jnp.zeros((24, 64), F32)
    for k in range(3):
        stage[8 * k : 8 * k + 4] = w1_ref[k].astype(F32)
    w1t = (0.5 * transposed(stage[...].astype(BF16))).astype(BF16)

    row = iota((24, 32), 0)
    col = iota((24, 32), 1)
    same_field = (row & 7) == ((col & 7) >> 1)
    level_in = 2 * (col >> 3) + (col & 1)
    for j in range(6):
        tap = one(jnp.logical_and(same_field, level_in == j + (row >> 3))).astype(BF16)
        band1[64 * j : 64 * j + 64] = dot(w1t, tap).astype(BF16)
    zeros = jnp.zeros((64, 64), F32)
    for w_ref, band_ref in ((w2_ref, band2), (w3_ref, band3)):
        taps = [0.5 * transposed(w_ref[k]) for k in range(3)]
        for o in range(2):
            parts = [taps[i - o] if 0 <= i - o < 3 else zeros for i in range(4)]
            band_ref[64 * o : 64 * o + 64] = jnp.concatenate(parts, axis=1).astype(BF16)
    rho = iota((16, 64), 0)
    level_out = 2 * (rho >> 3) + (rho & 1)
    stage[0:8] = jnp.zeros((8, 64), F32)
    pick = one(iota((16, 8), 1) == ((iota((16, 8), 0) & 7) >> 1)).astype(BF16)
    last = []
    for k in range(3):
        stage[0:4] = w4_ref[k].astype(F32)
        last.append(dot(pick, stage[0:8].astype(BF16)))
    for t in range(2):
        parts = []
        for i in range(4):
            part = jnp.zeros((16, 64), F32)
            for k in range(3):
                part = part + jnp.where(level_out == 4 * t + i - k, last[k], 0.0)
            parts.append(part)
        wd[t] = jnp.concatenate(parts, axis=1).astype(BF16)

    @pl.when(jnp.logical_not(at_south))
    def _():
        to_north.wait_recv()

    @pl.when(jnp.logical_not(at_north))
    def _():
        to_south.wait_recv()

    first_transport(0, NCH - 1, {1: jnp.where(at_south, 0.0, 1.0).astype(F32)})
    first_transport(3, NCH - 1, {2: jnp.where(at_north, 0.0, 1.0).astype(F32)})
    for k in (0, 3):
        send_x(k, NCH - 1)

    def forward(up, c):
        src, dst = (G, 0) if up else (2, G + 2)
        return pltpu.make_async_remote_copy(
            xbuf.at[pl.ds(src, 2), pl.ds(base_of(c), CH)],
            xbuf.at[pl.ds(dst, 2), pl.ds(base_of(c), CH)],
            f_send.at[int(up), c],
            f_recv.at[int(up), c],
            device_id=(lat, wide + G if up else wide - G),
            device_id_type=MESH,
        )

    low_valid = jnp.where(grp == 0, 0.0, 1.0).astype(F32)
    high_valid = jnp.where(grp == n_groups - 1, 0.0, 1.0).astype(F32)

    def t_copy(k, c):
        return pltpu.make_async_remote_copy(
            tsend.at[k, pl.ds(base_of(c), CH)],
            tin.at[m, pl.ds(base_of(c), CH)],
            t_send.at[k, c],
            t_recv.at[m, c],
            device_id=(lat, grp * G + k),
            device_id_type=MESH,
        )

    def store_act(dst, src, at, z, low, high):
        halves = ((0, 128, None),)
        if low is not None or high is not None:
            halves = ((0, 64, low), (64, 64, high))
        for o, size, valid in halves:
            part = z[o : o + size]
            if valid is not None:
                part = part * valid
            out = act(part)
            if src is not None:
                out = src[at + o + 64 : at + o + 64 + size].astype(F32) + out
            dst[at + o : at + o + size] = out.astype(BF16)

    def first_stage(r, slab, pairs, masks):
        parts = [xbuf[s, r].astype(F32) for s in range(slab, slab + 4)]
        x = jnp.concatenate(parts, axis=0).astype(BF16)
        for p in pairs:
            at = 128 * (p - slab)
            z = dot(band1[at : at + 128], x)
            store_act(h1.at[r], None, 128 * p, z, *masks.get(p, (None, None)))

    def later_stage(dst, src, band, r, pairs, masks):
        for p in pairs:
            at = 128 * p
            z = dot(band[...], src[r, at : at + 256])
            store_act(dst.at[r], src.at[r], at, z, *masks.get(p, (None, None)))

    def finish(r, p, members):
        at = 64 * p
        out = dot(wd[0], h3[r, at : at + 256]) + dot(wd[1][:, 0:128], h3[r, at + 256 : at + 384])
        for n, k in enumerate(members):
            tsend[k, r] = out[8 * n : 8 * n + 8].astype(BF16)

    def send_t(members, c):
        for k in members:
            @pl.when(m != k)
            def _():
                t_copy(k, c).start()

    def rows_of(chunks):
        return [base_of(c) + i for c in chunks for i in range(CH)]

    mine = (25 * m + 1) // 3

    def relay(c):
        xbuf[pl.ds(m + 2, 1), pl.ds(base_of(c), CH)] = packed[pl.ds(mine + base_of(c), CH)][None]
        for k in range(G):
            @pl.when(m != k)
            def _():
                pltpu.make_async_remote_copy(
                    packed.at[pl.ds(0, CH)], xbuf.at[k + 2, pl.ds(base_of(c), CH)],
                    x_send.at[k, c], x_recv.at[k, c],
                    device_id=(lat, wide), device_id_type=MESH,
                ).wait_recv()

        @pl.when(has_high)
        def _():
            forward(True, c).start()

        @pl.when(has_low)
        def _():
            if c == 0:
                pl.semaphore_wait(ready, 1)
            forward(False, c).start()

    def middle(c):
        rows = rows_of((c,))
        for r in rows:
            first_stage(r, 2, (2, 3, 4), {})
        for r in rows:
            later_stage(h2, h1, band2, r, (2, 3), {})
        for r in rows:
            later_stage(h3, h2, band3, r, (2,), {})

    relay(0)
    relay(1)
    middle(0)
    relay(2)
    middle(1)
    middle(2)

    def upper(chunks):
        for c in chunks:
            @pl.when(has_high)
            def _():
                forward(False, c).wait_recv()

        rows = rows_of(chunks)
        for r in rows:
            first_stage(r, 4, (5, 6), {5: (None, high_valid), 6: (high_valid, high_valid)})
        for r in rows:
            later_stage(h2, h1, band2, r, (4, 5), {5: (high_valid, high_valid)})
        for r in rows:
            later_stage(h3, h2, band3, r, (3, 4), {4: (None, high_valid)})
        for r in rows:
            finish(r, 4, (2, 3))
        for c in chunks:
            send_t((2, 3), c)

    def lower(chunks):
        for c in chunks:
            @pl.when(has_low)
            def _():
                forward(True, c).wait_recv()

        rows = rows_of(chunks)
        for r in rows:
            first_stage(r, 0, (0, 1), {0: (low_valid, low_valid), 1: (low_valid, None)})
        for r in rows:
            later_stage(h2, h1, band2, r, (0, 1), {0: (low_valid, low_valid)})
        for r in rows:
            later_stage(h3, h2, band3, r, (0, 1), {0: (low_valid, None)})
        for r in rows:
            finish(r, 0, (0, 1))
        for c in chunks:
            send_t((0, 1), c)

    for chunks in UPPER:
        upper(chunks)
    for chunks in LOWER:
        lower(chunks)
    tin[pl.ds(m, 1)] = tsend[pl.ds(m, 1)]

    for k in range(G):
        @pl.when(m != k)
        def _():
            for c in range(NCH):
                pltpu.make_async_remote_copy(
                    tsend.at[k, pl.ds(local_row(k, c), CH)],
                    tin.at[k, pl.ds(local_row(k, c), CH)],
                    t_send.at[k, c], t_recv.at[k, c],
                    device_id=(lat, wide), device_id_type=MESH,
                ).wait_recv()

        first = STARTS[k] if k == 0 else STARTS[k - 1] + R
        for e in range(first, STARTS[k] + R):
            upd_ref[e] = adv[e] + tin[k, e - STARTS[k]].astype(F32)

    @pl.when(jnp.logical_not(at_north))
    def _():
        to_north.wait_send()

    @pl.when(jnp.logical_not(at_south))
    def _():
        to_south.wait_send()

    for c in range(NCH):
        @pl.when(has_high)
        def _():
            forward(True, c).wait_send()

        @pl.when(has_low)
        def _():
            forward(False, c).wait_send()

        for k in range(G):
            @pl.when(m != k)
            def _():
                x_copy(k, c).wait_send()
                t_copy(k, c).wait_send()


def second_kernel(upd_ref, out_ref, outv, sem):
    lat = lax.axis_index("lat")
    at_south = lat == 0
    at_north = lat == lax.axis_size("lat") - 1
    stores = []
    for c in range(4):
        masks = {}
        if c == 0:
            masks = {0: jnp.where(at_south, 0.0, 1.0).astype(F32)}
        if c == 3:
            masks = {8: jnp.where(at_north, 0.0, 1.0).astype(F32)}
        e = 8 * c
        outs = transport([upd_ref[e + i] for i in range(10)], masks)
        for i in range(8):
            outv[e + i] = outs[i]
        for f in range(4):
            for l in range(2):
                d = pltpu.make_async_copy(
                    outv.at[pl.ds(e, 8), 2 * f + l],
                    out_ref.at[f, l, pl.ds(e, 8)],
                    sem.at[c, 2 * f + l],
                )
                d.start()
                stores.append(d)
    for d in stores:
        d.wait()


def on_device(fields, w_first, w_second, w_third, w_last):
    anywhere = pl.BlockSpec(memory_space=pltpu.HBM)
    vmem = pl.BlockSpec(memory_space=pltpu.VMEM)
    dma = pltpu.SemaphoreType.DMA
    arguments = (fields, w_first, w_second, w_third, jnp.transpose(w_last, (0, 2, 1)))
    updated = pl.pallas_call(
        kernel,
        out_shape=jax.ShapeDtypeStruct((34, 8, 256), F32),
        in_specs=[anywhere] * 5,
        out_specs=vmem,
        scratch_shapes=[
            pltpu.VMEM((36, 8, 256), F32),
            pltpu.VMEM((34, 8, 256), F32),
            pltpu.VMEM((34, 8, 256), BF16),
            pltpu.VMEM((SLABS, R, 8, 256), BF16),
            pltpu.VMEM((G, R, 8, 256), BF16),
            pltpu.VMEM((G, R, 8, 256), BF16),
            pltpu.VMEM((3, 4, 64), BF16),
            pltpu.VMEM((3, 64, 64), BF16),
            pltpu.VMEM((3, 64, 64), BF16),
            pltpu.VMEM((3, 4, 64), BF16),
            pltpu.VMEM((6 * 64, 32), BF16),
            pltpu.VMEM((2 * 64, 256), BF16),
            pltpu.VMEM((2 * 64, 256), BF16),
            pltpu.VMEM((2, 16, 256), BF16),
            pltpu.VMEM((24, 64), F32),
            pltpu.VMEM((R, 14 * 64, 256), BF16),
            pltpu.VMEM((R, 12 * 64, 256), BF16),
            pltpu.VMEM((R, 10 * 64, 256), BF16),
            dma((8,)),
            dma((4,)),
            dma((2,)),
            dma((2,)),
            dma((G, NCH)),
            dma((G, NCH)),
            dma((2, NCH)),
            dma((2, NCH)),
            dma((G, NCH)),
            dma((G, NCH)),
            pltpu.SemaphoreType.REGULAR,
        ],
        compiler_params=pltpu.CompilerParams(
            collective_id=0, has_side_effects=True, vmem_limit_bytes=32 * 1024 * 1024
        ),
        name="climate_step",
    )(*[pltpu.with_memory_space_constraint(v, pltpu.HBM) for v in arguments])
    return pl.pallas_call(
        second_kernel,
        out_shape=jax.ShapeDtypeStruct(fields.shape, F32),
        in_specs=[vmem],
        out_specs=anywhere,
        scratch_shapes=[pltpu.VMEM((32, 8, 256), F32), dma((4, 8))],
        compiler_params=pltpu.CompilerParams(vmem_limit_bytes=8 * 1024 * 1024),
        name="climate_end",
    )(updated)


def solution(mesh):
    return jax.shard_map(
        on_device,
        mesh=mesh,
        in_specs=(P(None, "wide", "lat", None), P(), P(), P(), P()),
        out_specs=P(None, "wide", "lat", None),
        check_vma=False,
    )
```

time: 25.5 us -> 24 us (0.941)
  Pallas kernels: 25.4 us -> 23.8 us
    pallas_call x1, Pallas kernels: 23.7 us -> 22.1 us  [on_device(): pl.pallas_call(kernel, out_shape=jax.ShapeDtypeStruct((34, 8, 256), F32),...]
where the time goes in v3:
time: 24 us; the launch traced here: 23.9 us
  Pallas kernels  23.8 us (99%)
    pallas_call x1, Pallas kernels, on_device(): pl.pallas_call(kernel, out_shape=jax.ShapeDtypeStruct((34, 8, 256), F32),...  22.1 us
    pallas_call x1, Pallas kernels, on_device(): pl.pallas_call(second_kernel, out_shape=jax.ShapeDtypeStruct(fields.shape...  1.71 us

profile of v3, /device:TPU:6, one launch (start us, length us, event | category | flops | bytes accessed | tf_op | source)
XLA Modules:
  0.0 23.9 jit_solution(18418569118584423372)
XLA Ops:
  0.0 22.1 %climate_step.1.upd_ref = f32[34,8,256]{2,1,0:T(8,128)S(1)} custom-call(f32[4,2,32,256]{3,2,1,0:T(8,128)} %f_hbm.1, bf16[3,4,64]{2,1,0:T(4,128)(2,1)} %w1_hbm.1, bf16[3,64,64]{2,1,0:T(8,128)(2,1)} %w2_hbm.1, bf16[3,64,64]{2,1,0:T(8,128)(2,1)} %w3_hbm.1, bf16[3,4,64]{2,1,0:T(4,128)(2,1)} %bitcast.1), custom_call_target="tpu_custom_call" | custom-call | tf_op jit(solution)/shard_map/climate_step/pallas_call | solution.py:500
  22.1 1.7 %climate_end.1 = f32[4,2,32,256]{3,2,1,0:T(8,128)} custom-call(f32[34,8,256]{2,1,0:T(8,128)S(1)} %climate_step.1.upd_ref), custom_call_target="tpu_custom_call" | custom-call | tf_op jit(solution)/shard_map/climate_end/pallas_call | solution.py:541

commit v4 on v3

--- a/solution.py
+++ b/solution.py
@@ -82,6 +82,15 @@
     at_north = lat == n_lat - 1
     has_low = grp > 0
     has_high = grp < n_groups - 1
+    cross_low = grp == n_groups // 2
+    cross_high = grp == n_groups // 2 - 1
+    up = m >= 2
+    down = jnp.logical_and(has_low, jnp.logical_not(cross_low))
+    has_other = jnp.logical_or(
+        jnp.logical_and(up, has_high), jnp.logical_and(jnp.logical_not(up), down)
+    )
+    og = jnp.where(up, grp + 1, grp - 1)
+    os = jnp.where(up, m - 2, m + G + 2)
 
     barrier = pltpu.get_barrier_semaphore()
 
@@ -89,6 +98,16 @@
         pl.semaphore_signal(barrier, inc=1, device_id=(la, wi), device_id_type=MESH)
 
     @pl.when(has_low)
+    def _():
+        for k in (2, 3):
+            greet(lat, (grp - 1) * G + k)
+
+    @pl.when(jnp.logical_and(has_high, jnp.logical_not(cross_high)))
+    def _():
+        for k in (0, 1):
+            greet(lat, (grp + 1) * G + k)
+
+    @pl.when(jnp.logical_and(cross_low, jnp.logical_not(up)))
     def _():
         greet(lat, wide - G)
 
@@ -157,21 +176,35 @@
             adv[e + i] = outs[i]
             packed[e + i] = outs[i].astype(BF16)
 
-    def x_copy(k, c):
+    def x_copy(k, c, group, slab, other):
         row = local_row(k, c)
         return pltpu.make_async_remote_copy(
             packed.at[pl.ds(STARTS[k] + row, CH)],
-            xbuf.at[m + 2, pl.ds(row, CH)],
-            x_send.at[k, c],
-            x_recv.at[m, c],
-            device_id=(lat, grp * G + k),
+            xbuf.at[slab, pl.ds(row, CH)],
+            x_send.at[other, k, c],
+            x_recv.at[slab, c],
+            device_id=(lat, group * G + k),
             device_id_type=MESH,
         )
 
-    def send_x(k, c):
+    def each_x(k, c, act_on):
+        @pl.when(has_other)
+        def _():
+            act_on(x_copy(k, c, og, os, 1))
+
         @pl.when(m != k)
         def _():
-            x_copy(k, c).start()
+            act_on(x_copy(k, c, grp, m + 2, 0))
+
+    def send_x(k, c):
+        each_x(k, c, lambda d: d.start())
+
+    def x_arrived(slab, c):
+        pltpu.make_async_remote_copy(
+            packed.at[pl.ds(0, CH)], xbuf.at[slab, pl.ds(base_of(c), CH)],
+            x_send.at[0, 0, c], x_recv.at[slab, c],
+            device_id=(lat, wide), device_id_type=MESH,
+        ).wait_recv()
 
     for k in range(G):
         first_transport(k, 0, {})
@@ -180,11 +213,12 @@
         (G - 1)
         + jnp.where(at_south, 0, 1)
         + jnp.where(at_north, 0, 1)
-        + jnp.where(has_high, 1, 0)
+        + jnp.where(has_other, G, 0)
+        + jnp.where(jnp.logical_and(cross_high, jnp.logical_not(up)), 1, 0)
     )
     pl.semaphore_wait(barrier, expected)
 
-    @pl.when(has_high)
+    @pl.when(cross_high)
     def _():
         pl.semaphore_signal(ready, inc=1, device_id=(lat, wide + G), device_id_type=MESH)
 
@@ -278,14 +312,13 @@
     for k in (0, 3):
         send_x(k, NCH - 1)
 
-    def forward(up, c):
-        src, dst = (G, 0) if up else (2, G + 2)
+    def forward(c):
         return pltpu.make_async_remote_copy(
-            xbuf.at[pl.ds(src, 2), pl.ds(base_of(c), CH)],
-            xbuf.at[pl.ds(dst, 2), pl.ds(base_of(c), CH)],
-            f_send.at[int(up), c],
-            f_recv.at[int(up), c],
-            device_id=(lat, wide + G if up else wide - G),
+            xbuf.at[pl.ds(2, 2), pl.ds(base_of(c), CH)],
+            xbuf.at[pl.ds(G + 2, 2), pl.ds(base_of(c), CH)],
+            f_send.at[c],
+            f_recv.at[c],
+            device_id=(lat, wide - G),
             device_id_type=MESH,
         )
 
@@ -351,21 +384,13 @@
         for k in range(G):
             @pl.when(m != k)
             def _():
-                pltpu.make_async_remote_copy(
-                    packed.at[pl.ds(0, CH)], xbuf.at[k + 2, pl.ds(base_of(c), CH)],
-                    x_send.at[k, c], x_recv.at[k, c],
-                    device_id=(lat, wide), device_id_type=MESH,
-                ).wait_recv()
-
-        @pl.when(has_high)
-        def _():
-            forward(True, c).start()
-
-        @pl.when(has_low)
+                x_arrived(k + 2, c)
+
+        @pl.when(cross_low)
         def _():
             if c == 0:
                 pl.semaphore_wait(ready, 1)
-            forward(False, c).start()
+            forward(c).start()
 
     def middle(c):
         rows = rows_of((c,))
@@ -385,9 +410,14 @@
 
     def upper(chunks):
         for c in chunks:
-            @pl.when(has_high)
+            @pl.when(cross_high)
             def _():
-                forward(False, c).wait_recv()
+                forward(c).wait_recv()
+
+            @pl.when(jnp.logical_and(has_high, jnp.logical_not(cross_high)))
+            def _():
+                x_arrived(G + 2, c)
+                x_arrived(G + 3, c)
 
         rows = rows_of(chunks)
         for r in rows:
@@ -405,7 +435,8 @@
         for c in chunks:
             @pl.when(has_low)
             def _():
-                forward(True, c).wait_recv()
+                x_arrived(0, c)
+                x_arrived(1, c)
 
         rows = rows_of(chunks)
         for r in rows:
@@ -449,18 +480,15 @@
         to_south.wait_send()
 
     for c in range(NCH):
-        @pl.when(has_high)
+        @pl.when(cross_low)
         def _():
-            forward(True, c).wait_send()
-
-        @pl.when(has_low)
-        def _():
-            forward(False, c).wait_send()
+            forward(c).wait_send()
 
         for k in range(G):
+            each_x(k, c, lambda d: d.wait_send())
+
             @pl.when(m != k)
             def _():
-                x_copy(k, c).wait_send()
                 t_copy(k, c).wait_send()
 
 
@@ -525,10 +553,10 @@
             dma((4,)),
             dma((2,)),
             dma((2,)),
-            dma((G, NCH)),
-            dma((G, NCH)),
-            dma((2, NCH)),
-            dma((2, NCH)),
+            dma((2, G, NCH)),
+            dma((SLABS, NCH)),
+            dma((NCH,)),
+            dma((NCH,)),
             dma((G, NCH)),
             dma((G, NCH)),
             pltpu.SemaphoreType.REGULAR,

time: 24 us -> 22.7 us (0.946)
  Pallas kernels: 23.8 us -> 22.5 us
    pallas_call x1, Pallas kernels: 22.1 us -> 20.8 us  [on_device(): pl.pallas_call(kernel, out_shape=jax.ShapeDtypeStruct((34, 8, 256), F32),...]
where the time goes in v4:
time: 22.7 us; the launch traced here: 22.5 us
  Pallas kernels  22.5 us (99%)
    pallas_call x1, Pallas kernels, on_device(): pl.pallas_call(kernel, out_shape=jax.ShapeDtypeStruct((34, 8, 256), F32),...  20.8 us
    pallas_call x1, Pallas kernels, on_device(): pl.pallas_call(second_kernel, out_shape=jax.ShapeDtypeStruct(fields.shape...  1.71 us

profile of v4, /device:TPU:6, one launch (start us, length us, event | category | flops | bytes accessed | tf_op | source)
XLA Modules:
  0.0 22.5 jit_solution(13391466758601017006)
XLA Ops:
  0.0 20.8 %climate_step.1.upd_ref = f32[34,8,256]{2,1,0:T(8,128)S(1)} custom-call(f32[4,2,32,256]{3,2,1,0:T(8,128)} %f_hbm.1, bf16[3,4,64]{2,1,0:T(4,128)(2,1)} %w1_hbm.1, bf16[3,64,64]{2,1,0:T(8,128)(2,1)} %w2_hbm.1, bf16[3,64,64]{2,1,0:T(8,128)(2,1)} %w3_hbm.1, bf16[3,4,64]{2,1,0:T(4,128)(2,1)} %bitcast.1), custom_call_target="tpu_custom_call" | custom-call | tf_op jit(solution)/shard_map/climate_step/pallas_call | solution.py:528
  20.8 1.7 %climate_end.1 = f32[4,2,32,256]{3,2,1,0:T(8,128)} custom-call(f32[34,8,256]{2,1,0:T(8,128)S(1)} %climate_step.1.upd_ref), custom_call_target="tpu_custom_call" | custom-call | tf_op jit(solution)/shard_map/climate_end/pallas_call | solution.py:569

commit v5 on v4

--- a/solution.py
+++ b/solution.py
@@ -15,7 +15,7 @@
 CH = 3
 NCH = R // CH
 SLABS = G + 4
-UPPER = ((0,), (1,), (2,))
+UPPER = ((0, 1, 2),)
 LOWER = ((0,), (1,), (2,))
 
 
@@ -348,23 +348,25 @@
                 out = src[at + o + 64 : at + o + 64 + size].astype(F32) + out
             dst[at + o : at + o + size] = out.astype(BF16)
 
-    def first_stage(r, slab, pairs, masks):
+    def first_stage(row, slab, pairs, masks):
+        r, at_row = row
         parts = [xbuf[s, r].astype(F32) for s in range(slab, slab + 4)]
         x = jnp.concatenate(parts, axis=0).astype(BF16)
         for p in pairs:
             at = 128 * (p - slab)
             z = dot(band1[at : at + 128], x)
-            store_act(h1.at[r], None, 128 * p, z, *masks.get(p, (None, None)))
-
-    def later_stage(dst, src, band, r, pairs, masks):
+            store_act(h1.at[at_row], None, 128 * p, z, *masks.get(p, (None, None)))
+
+    def later_stage(dst, src, band, row, pairs, masks):
         for p in pairs:
             at = 128 * p
-            z = dot(band[...], src[r, at : at + 256])
-            store_act(dst.at[r], src.at[r], at, z, *masks.get(p, (None, None)))
-
-    def finish(r, p, members):
+            z = dot(band[...], src[row[1], at : at + 256])
+            store_act(dst.at[row[1]], src.at[row[1]], at, z, *masks.get(p, (None, None)))
+
+    def finish(row, p, members):
+        r, n_row = row
         at = 64 * p
-        out = dot(wd[0], h3[r, at : at + 256]) + dot(wd[1][:, 0:128], h3[r, at + 256 : at + 384])
+        out = dot(wd[0], h3[n_row, at : at + 256]) + dot(wd[1][:, 0:128], h3[n_row, at + 256 : at + 384])
         for n, k in enumerate(members):
             tsend[k, r] = out[8 * n : 8 * n + 8].astype(BF16)
 
@@ -375,7 +377,7 @@
                 t_copy(k, c).start()
 
     def rows_of(chunks):
-        return [base_of(c) + i for c in chunks for i in range(CH)]
+        return [(base_of(c) + i, CH * c + i) for c in chunks for i in range(CH)]
 
     mine = (25 * m + 1) // 3
 

time: 22.7 us -> 21.7 us (0.956)
  Pallas kernels: 22.5 us -> 21.5 us
    pallas_call x1, Pallas kernels: 20.8 us -> 19.8 us  [on_device(): pl.pallas_call(kernel, out_shape=jax.ShapeDtypeStruct((34, 8, 256), F32),...]
where the time goes in v5:
time: 21.7 us; the launch traced here: 21.5 us
  Pallas kernels  21.5 us (99%)
    pallas_call x1, Pallas kernels, on_device(): pl.pallas_call(kernel, out_shape=jax.ShapeDtypeStruct((34, 8, 256), F32),...  19.8 us
    pallas_call x1, Pallas kernels, on_device(): pl.pallas_call(second_kernel, out_shape=jax.ShapeDtypeStruct(fields.shape...  1.71 us

profile of v5, /device:TPU:6, one launch (start us, length us, event | category | flops | bytes accessed | tf_op | source)
XLA Modules:
  0.0 21.5 jit_solution(4627655286100027384)
XLA Ops:
  0.0 19.8 %climate_step.1.upd_ref = f32[34,8,256]{2,1,0:T(8,128)S(1)} custom-call(f32[4,2,32,256]{3,2,1,0:T(8,128)} %f_hbm.1, bf16[3,4,64]{2,1,0:T(4,128)(2,1)} %w1_hbm.1, bf16[3,64,64]{2,1,0:T(8,128)(2,1)} %w2_hbm.1, bf16[3,64,64]{2,1,0:T(8,128)(2,1)} %w3_hbm.1, bf16[3,4,64]{2,1,0:T(4,128)(2,1)} %bitcast.1), custom_call_target="tpu_custom_call" | custom-call | tf_op jit(solution)/shard_map/climate_step/pallas_call | solution.py:530
  19.8 1.7 %climate_end.1 = f32[4,2,32,256]{3,2,1,0:T(8,128)} custom-call(f32[34,8,256]{2,1,0:T(8,128)S(1)} %climate_step.1.upd_ref), custom_call_target="tpu_custom_call" | custom-call | tf_op jit(solution)/shard_map/climate_end/pallas_call | solution.py:571

commit v6 on v5

--- a/solution.py
+++ b/solution.py
@@ -16,7 +16,7 @@
 NCH = R // CH
 SLABS = G + 4
 UPPER = ((0, 1, 2),)
-LOWER = ((0,), (1,), (2,))
+LOWER = ((0, 1), (2,))
 
 
 def face_terms(total):
@@ -394,8 +394,8 @@
                 pl.semaphore_wait(ready, 1)
             forward(c).start()
 
-    def middle(c):
-        rows = rows_of((c,))
+    def middle(chunks):
+        rows = rows_of(chunks)
         for r in rows:
             first_stage(r, 2, (2, 3, 4), {})
         for r in rows:
@@ -405,10 +405,9 @@
 
     relay(0)
     relay(1)
-    middle(0)
+    middle((0, 1))
     relay(2)
-    middle(1)
-    middle(2)
+    middle((2,))
 
     def upper(chunks):
         for c in chunks:

time: 21.7 us -> 21.5 us (level)
  no operation moved by 1% of the time
where the time goes in v6:
time: 21.5 us; the launch traced here: 21.4 us
  Pallas kernels  21.4 us (100%)
    pallas_call x1, Pallas kernels, on_device(): pl.pallas_call(kernel, out_shape=jax.ShapeDtypeStruct((34, 8, 256), F32),...  19.6 us
    pallas_call x1, Pallas kernels, on_device(): pl.pallas_call(second_kernel, out_shape=jax.ShapeDtypeStruct(fields.shape...  1.71 us

profile of v6, /device:TPU:6, one launch (start us, length us, event | category | flops | bytes accessed | tf_op | source)
XLA Modules:
  0.0 21.4 jit_solution(2362320682060277388)
XLA Ops:
  0.0 19.6 %climate_step.1.upd_ref = f32[34,8,256]{2,1,0:T(8,128)S(1)} custom-call(f32[4,2,32,256]{3,2,1,0:T(8,128)} %f_hbm.1, bf16[3,4,64]{2,1,0:T(4,128)(2,1)} %w1_hbm.1, bf16[3,64,64]{2,1,0:T(8,128)(2,1)} %w2_hbm.1, bf16[3,64,64]{2,1,0:T(8,128)(2,1)} %w3_hbm.1, bf16[3,4,64]{2,1,0:T(4,128)(2,1)} %bitcast.1), custom_call_target="tpu_custom_call" | custom-call | tf_op jit(solution)/shard_map/climate_step/pallas_call | solution.py:529
  19.7 1.7 %climate_end.1 = f32[4,2,32,256]{3,2,1,0:T(8,128)} custom-call(f32[34,8,256]{2,1,0:T(8,128)S(1)} %climate_step.1.upd_ref), custom_call_target="tpu_custom_call" | custom-call | tf_op jit(solution)/shard_map/climate_end/pallas_call | solution.py:570

commit v7 on v6

--- a/solution.py
+++ b/solution.py
@@ -457,6 +457,26 @@
         lower(chunks)
     tin[pl.ds(m, 1)] = tsend[pl.ds(m, 1)]
 
+    @pl.when(jnp.logical_not(at_north))
+    def _():
+        to_north.wait_send()
+
+    @pl.when(jnp.logical_not(at_south))
+    def _():
+        to_south.wait_send()
+
+    for c in range(NCH):
+        @pl.when(cross_low)
+        def _():
+            forward(c).wait_send()
+
+        for k in range(G):
+            each_x(k, c, lambda d: d.wait_send())
+
+            @pl.when(m != k)
+            def _():
+                t_copy(k, c).wait_send()
+
     for k in range(G):
         @pl.when(m != k)
         def _():
@@ -471,26 +491,6 @@
         first = STARTS[k] if k == 0 else STARTS[k - 1] + R
         for e in range(first, STARTS[k] + R):
             upd_ref[e] = adv[e] + tin[k, e - STARTS[k]].astype(F32)
-
-    @pl.when(jnp.logical_not(at_north))
-    def _():
-        to_north.wait_send()
-
-    @pl.when(jnp.logical_not(at_south))
-    def _():
-        to_south.wait_send()
-
-    for c in range(NCH):
-        @pl.when(cross_low)
-        def _():
-            forward(c).wait_send()
-
-        for k in range(G):
-            each_x(k, c, lambda d: d.wait_send())
-
-            @pl.when(m != k)
-            def _():
-                t_copy(k, c).wait_send()
 
 
 def second_kernel(upd_ref, out_ref, outv, sem):

time: 21.5 us -> 21.5 us (level)
  no operation moved by 1% of the time
where the time goes in v7:
time: 21.5 us; the launch traced here: 21.3 us
  Pallas kernels  21.3 us (99%)
    pallas_call x1, Pallas kernels, on_device(): pl.pallas_call(kernel, out_shape=jax.ShapeDtypeStruct((34, 8, 256), F32),...  19.6 us
    pallas_call x1, Pallas kernels, on_device(): pl.pallas_call(second_kernel, out_shape=jax.ShapeDtypeStruct(fields.shape...  1.71 us

profile of v7, /device:TPU:6, one launch (start us, length us, event | category | flops | bytes accessed | tf_op | source)
XLA Modules:
  0.0 21.3 jit_solution(6551774793888332320)
XLA Ops:
  0.0 19.6 %climate_step.1.upd_ref = f32[34,8,256]{2,1,0:T(8,128)S(1)} custom-call(f32[4,2,32,256]{3,2,1,0:T(8,128)} %f_hbm.1, bf16[3,4,64]{2,1,0:T(4,128)(2,1)} %w1_hbm.1, bf16[3,64,64]{2,1,0:T(8,128)(2,1)} %w2_hbm.1, bf16[3,64,64]{2,1,0:T(8,128)(2,1)} %w3_hbm.1, bf16[3,4,64]{2,1,0:T(4,128)(2,1)} %bitcast.1), custom_call_target="tpu_custom_call" | custom-call | tf_op jit(solution)/shard_map/climate_step/pallas_call | solution.py:529
  19.6 1.7 %climate_end.1 = f32[4,2,32,256]{3,2,1,0:T(8,128)} custom-call(f32[34,8,256]{2,1,0:T(8,128)S(1)} %climate_step.1.upd_ref), custom_call_target="tpu_custom_call" | custom-call | tf_op jit(solution)/shard_map/climate_end/pallas_call | solution.py:570
